TPU v7x, 256 devices: a whole 4x4x8 slice. The times are simulated.
256 devices in a mesh: ctx: 128 (over z, x, y_hi, core), head: 2 (over y_lo).
Axes of the slice: x: 4, y: 4 (y_hi: 2, y_lo: 2; y = y_hi * 2 + y_lo), z: 8, core: 2. Of those that a mesh axis runs over, the one named last changes fastest.
Arguments:
- fw_q: bfloat16 [32768, 2048], P('ctx', 'head'), may hold values from -6 to 6
- fw_k: bfloat16 [32768, 2048], P('ctx', 'head'), may hold values from -16 to 16
- fw_v: bfloat16 [32768, 2048], P('ctx', 'head'), may hold values from -6 to 6
- fw_lr: float32 [32768, 4], P('ctx', 'head'), may hold values from 0.1 to 3
- fast_gate: bfloat16 [4, 512, 512], P('head'), may hold values from -0.25 to 0.25
- fast_up: bfloat16 [4, 512, 512], P('head'), may hold values from -0.25 to 0.25
- fast_down: bfloat16 [4, 512, 512], P('head'), may hold values from -0.25 to 0.25
- attn_q: bfloat16 [32768, 2048], P('ctx', 'head'), may hold values from -96 to 96
- attn_k: bfloat16 [32768, 2048], P('ctx', 'head'), may hold values from -10 to 10
- attn_v: bfloat16 [32768, 2048], P('ctx', 'head'), may hold values from -6 to 6
Outputs:
- mixed_out: bfloat16 [32768, 2048], P(('ctx', 'head'))
All inputs are finite; a program needn't handle non-finite values.
Results may differ from a plain program's by a relative error of at most 0.0095.
Values may be sent and summed in bfloat16 or wider, within the bound.
No kernel may reach another device: no remote copies, remote signals or barrier semaphores. Data moves between devices by JAX's collectives and lax.ppermute only.
A program may use at most 128 MiB of HBM per device.

v0:
```python
import math

import jax
import jax.numpy as jnp
from jax import lax
from jax.experimental import pallas as pl
from jax.experimental.pallas import tpu as pltpu
from jax.sharding import Mesh, PartitionSpec as P

SWA_DH = 128
WINDOW = 128
NS_ITERS = 2
DH = 512
HALF = 256

linear_coef = 3.4445
square_coef = -4.775
quartic_coef = 2.0315
epsilon = 1e-06


CHIPS = ("z", "plane")
ORDERS = {"plane": [0, 5, 2, 7, 4, 1, 6, 3], "z": [0, 2, 4, 6, 1, 3, 5, 7]}
QUAD = ("core", "yl")

BF = jnp.bfloat16
F32 = jnp.float32
NN, NT, TN = ((1,), (0,)), ((1,), (1,)), ((0,), (0,))


def mat(left, right, dims):
    return lax.dot_general(left, right, (dims, ((), ())), preferred_element_type=F32)


def shape(dims, dtype=BF):
    return jax.ShapeDtypeStruct(dims, dtype)


def cost(flops, nbytes, trans=0):
    return pl.CostEstimate(flops=flops, bytes_accessed=nbytes, transcendentals=trans)


def vmem(value):
    return pltpu.with_memory_space_constraint(value, pltpu.VMEM)


def hbm(*values):
    return [pltpu.with_memory_space_constraint(v, pltpu.HBM) for v in values]


VM = pl.BlockSpec(memory_space=pltpu.VMEM)
SM = pl.BlockSpec(memory_space=pltpu.SMEM)
PARAMS = pltpu.CompilerParams(vmem_limit_bytes=24 * 1024 * 1024)


def on_chip(dims, dtype=BF):
    return pltpu.VMEM(dims, dtype)


HBM = pl.BlockSpec(memory_space=pltpu.HBM)


def half(ref, which):
    return ref.at[:, pl.ds(pl.multiple_of(which * DH, DH), DH)]


def start_all(pairs, sems):
    copies = [pltpu.make_async_copy(a, b, sems.at[i]) for i, (a, b) in enumerate(pairs)]
    for copy in copies:
        copy.start()
    return copies


def wait_all(copies):
    for copy in copies:
        copy.wait()


def pack_grad_body(core_ref, k_ref, v_ref, lr_ref, own_ref, send_ref, value_ref, rate_ref, sems):
    core = core_ref[0]
    rows = k_ref.shape[0]
    sides = ((send_ref, 1 - core), (own_ref, core))
    pairs = [(half(v_ref, which), value_ref.at[i]) for i, (_, which) in enumerate(sides)]
    pairs += [(half(k_ref, which), ref.at[0]) for ref, which in sides]
    copies = start_all([(lr_ref, rate_ref)] + pairs, sems)
    copies[0].wait()
    for i, (ref, which) in enumerate(sides):
        copies[1 + i].wait()
        rates = jnp.where(which == 0, rate_ref[0:1, :], rate_ref[1:2, :])
        rates = jnp.broadcast_to(rates, (SWA_DH, rows)).T
        for j in range(0, DH, SWA_DH):
            value = value_ref[i, :, j : j + SWA_DH].astype(F32)
            ref[1, :, j : j + SWA_DH] = (-(rates * value)).astype(BF)
    wait_all(copies[3:])


def pack_grad(core, fw_k, fw_v, fw_lr):
    rows = fw_k.shape[0]
    return pl.pallas_call(
        pack_grad_body,
        in_specs=[SM, HBM, HBM, HBM],
        out_specs=[VM, VM],
        out_shape=[on_chip((2, rows, DH)), on_chip((2, rows, DH))],
        scratch_shapes=[
            pltpu.VMEM((2, rows, DH), BF),
            pltpu.VMEM((2, rows), F32),
            pltpu.SemaphoreType.DMA((5,)),
        ],
        compiler_params=PARAMS,
        cost_estimate=cost(rows * 1024, 8 * rows * 1024),
        name="pack_grad",
    )(core, *hbm(fw_k, fw_v, fw_lr.T))


def pick_body(core_ref, gate_ref, up_ref, down_ref, out_ref, sems):
    pairs = [(w.at[core_ref[0]], out_ref.at[i]) for i, w in enumerate((gate_ref, up_ref, down_ref))]
    wait_all(start_all(pairs, sems))


def pick(core, weights):
    return pl.pallas_call(
        pick_body,
        in_specs=[SM] + [HBM] * 3,
        out_specs=VM,
        out_shape=on_chip((3, DH, DH)),
        scratch_shapes=[pltpu.SemaphoreType.DMA((3,))],
        compiler_params=PARAMS,
        cost_estimate=cost(0, 6 * DH * DH),
        name="pick",
    )(core, *hbm(*weights))


def pack_rest_body(core_ref, *refs):
    own_ref, send_ref, sems = refs[4:]
    core = core_ref[0]
    pairs = []
    for ref, which in ((send_ref, 1 - core), (own_ref, core)):
        pairs += [(half(source, which), ref.at[i]) for i, source in enumerate(refs[:4])]
    wait_all(start_all(pairs, sems))


def pack_rest(core, arrays):
    rows = arrays[0].shape[0]
    return pl.pallas_call(
        pack_rest_body,
        in_specs=[SM] + [HBM] * 4,
        out_specs=[VM, VM],
        out_shape=[shape((4, rows, DH)), shape((4, rows, DH))],
        scratch_shapes=[pltpu.SemaphoreType.DMA((8,))],
        compiler_params=PARAMS,
        cost_estimate=cost(0, 16 * rows * 1024),
        name="pack_rest",
    )(core, *hbm(*arrays))


def grads_body(own_ref, got_ref, weight_ref, out_ref):
    keys = jnp.concatenate([own_ref[0], got_ref[0]], axis=0)
    out_grad = jnp.concatenate([own_ref[1], got_ref[1]], axis=0)
    for h in range(DH // HALF):
        cols = slice(h * HALF, (h + 1) * HALF)
        pre_gate = mat(keys, weight_ref[0, :, cols], NN)
        pre_up = mat(keys, weight_ref[1, :, cols], NN)
        hidden_grad = mat(out_grad, weight_ref[2, cols, :], NT)
        sigmoid_gate = jax.nn.sigmoid(pre_gate)
        activated = pre_gate * sigmoid_gate
        hidden = (activated * pre_up).astype(BF)
        slope = sigmoid_gate * (1.0 + pre_gate * (1.0 - sigmoid_gate))
        gate_grad = (hidden_grad * pre_up * slope).astype(BF)
        up_grad = (hidden_grad * activated).astype(BF)
        out_ref[0, :, cols] = mat(keys, gate_grad, TN).astype(BF)
        out_ref[1, :, cols] = mat(keys, up_grad, TN).astype(BF)
        out_ref[2, cols, :] = mat(hidden, out_grad, TN).astype(BF)


def grads(own, got, weights):
    tokens = 2 * own.shape[1]
    return pl.pallas_call(
        grads_body,
        in_specs=[VM] * 3,
        out_specs=VM,
        out_shape=shape((3, DH, DH)),
        compiler_params=PARAMS,
        cost_estimate=cost(12 * tokens * DH * DH, 8 * DH * DH * 2, tokens * DH),
        name="grads",
    )(vmem(own), vmem(got), vmem(weights))


def add_up(in_ref, rows):
    total = in_ref[0, rows].astype(F32)
    for i in range(1, in_ref.shape[0]):
        total += in_ref[i, rows].astype(F32)
    return total.astype(BF)


def sum_body(in_ref, out_ref):
    for r in range(0, out_ref.shape[0], 16):
        rows = slice(r, r + 16)
        out_ref[rows] = add_up(in_ref, rows)


def plane_sum(parts):
    return pl.pallas_call(
        sum_body,
        in_specs=[VM],
        out_specs=VM,
        out_shape=shape(parts.shape[1:]),
        compiler_params=PARAMS,
        cost_estimate=cost(parts.size, 2 * parts.size),
        name="plane_sum",
    )(vmem(parts))


def sum_spread_body(in_ref, out_ref):
    total = add_up(in_ref, slice(None))
    for i in range(out_ref.shape[0]):
        out_ref[i] = total


def sum_spread(parts):
    return pl.pallas_call(
        sum_spread_body,
        in_specs=[VM],
        out_specs=VM,
        out_shape=shape(parts.shape),
        compiler_params=PARAMS,
        cost_estimate=cost(parts.size, 4 * parts.size),
        name="depth_sum",
    )(vmem(parts))


def attend_body(core_ref, chip_ref, own_ref, got_ref, halo_ref, out_ref, *scratch):
    q_ref, k_ref, v_ref, result_ref, sems, out_sem = scratch
    rows = own_ref.shape[1]
    pairs = [(halo_ref.at[0], k_ref.at[:WINDOW]), (halo_ref.at[1], v_ref.at[:WINDOW])]
    for source, which in ((own_ref, core_ref[0]), (got_ref, 1 - core_ref[0])):
        start = pl.multiple_of(which * rows, rows)
        pairs.append((source.at[1], q_ref.at[pl.ds(start, rows)]))
        pairs.append((source.at[2], k_ref.at[pl.ds(start + WINDOW, rows)]))
        pairs.append((source.at[3], v_ref.at[pl.ds(start + WINDOW, rows)]))
    wait_all(start_all(pairs, sems))
    scale = 1.0 / math.sqrt(SWA_DH)
    row = lax.broadcasted_iota(jnp.int32, (WINDOW, 2 * WINDOW), 0)
    col = lax.broadcasted_iota(jnp.int32, (WINDOW, 2 * WINDOW), 1)
    inside = (col > row) & (col <= row + WINDOW)
    first = inside & ((col >= WINDOW) | (chip_ref[0] > 0))
    for b in range(2 * rows // WINDOW):
        seen = first if b == 0 else inside
        queries = slice(b * WINDOW, (b + 1) * WINDOW)
        window = slice(b * WINDOW, (b + 2) * WINDOW)
        for h in range(DH // SWA_DH):
            cols = slice(h * SWA_DH, (h + 1) * SWA_DH)
            scores = mat(q_ref[queries, cols], k_ref[window, cols], NT) * scale
            scores = jnp.where(seen, scores, -jnp.inf)
            exponent = jnp.exp(scores - jnp.max(scores, axis=-1, keepdims=True))
            total = jnp.sum(exponent, axis=-1, keepdims=True)
            probs = (exponent * (1.0 / total)).astype(BF)
            result_ref[queries, cols] = mat(probs, v_ref[window, cols], NN)
    copy = pltpu.make_async_copy(result_ref, out_ref, out_sem)
    copy.start()
    copy.wait()


def attend(core, chip, own, got, halo):
    rows = own.shape[1]
    return pl.pallas_call(
        attend_body,
        in_specs=[SM, SM, HBM, HBM, HBM],
        out_specs=HBM,
        out_shape=pltpu.HBM((2 * rows, DH), F32),
        scratch_shapes=[
            pltpu.VMEM((2 * rows, DH), BF),
            pltpu.VMEM((2 * rows + WINDOW, DH), BF),
            pltpu.VMEM((2 * rows + WINDOW, DH), BF),
            pltpu.VMEM((2 * rows, DH), F32),
            pltpu.SemaphoreType.DMA((8,)),
            pltpu.SemaphoreType.DMA,
        ],
        compiler_params=PARAMS,
        cost_estimate=cost(2 * rows * 8 * WINDOW * DH, 12 * rows * DH, 4 * rows * DH),
        name="window_attention",
    )(core, chip, *hbm(own, got, halo))


def refresh(weight, update):
    initial = weight.astype(F32)
    stepped = initial - update.astype(F32)
    old_norm = jnp.sqrt(jnp.sum(initial * initial, axis=0, keepdims=True) + epsilon)
    new_norm = jnp.sqrt(jnp.sum(stepped * stepped, axis=0, keepdims=True) + epsilon)
    return (stepped * (old_norm / new_norm)).astype(BF)


def finish_body(
    core_ref, yl_ref, sum_ref, gate_ref, up_ref, down_ref, own_ref, got_ref, att_ref, *rest
):
    out_refs = rest[:4]
    all_ref, weight_ref, query_ref, attended_ref, sems = rest[4:]
    core, yl = core_ref[0], yl_ref[0]
    rows = own_ref.shape[1]
    pairs = [(w.at[core], weight_ref.at[i]) for i, w in enumerate((gate_ref, up_ref, down_ref))]
    pairs += [(own_ref.at[0], query_ref.at[0]), (got_ref.at[0], query_ref.at[1])]
    copies = start_all(pairs + [(att_ref, attended_ref)], sems)
    iterates = []
    for m in range(3):
        gradient = sum_ref[m].astype(F32)
        norm_total = jnp.sum(gradient * gradient)
        iterates.append((gradient * (1.0 / jnp.sqrt(norm_total + epsilon))).astype(BF))
    for _ in range(NS_ITERS):
        grams = [mat(x, x, NT).astype(BF) for x in iterates]
        polys = [
            (square_coef * g.astype(F32) + quartic_coef * mat(g, g, NN)).astype(BF) for g in grams
        ]
        iterates = [
            (linear_coef * x.astype(F32) + mat(p, x, NN)).astype(BF)
            for p, x in zip(polys, iterates)
        ]
    wait_all(copies)
    renewed = [refresh(weight_ref[i], x) for i, x in enumerate(iterates)]
    for i, start in enumerate((core * rows, (1 - core) * rows)):
        place = pl.ds(pl.multiple_of(start, rows), rows)
        query_gate = mat(query_ref[i], renewed[0], NN)
        query_up = mat(query_ref[i], renewed[1], NN)
        query_hidden = (query_gate * jax.nn.sigmoid(query_gate) * query_up).astype(BF)
        memory = mat(query_hidden, renewed[2], NN).astype(BF)
        all_ref[place] = (memory.astype(F32) + attended_ref[place]).astype(BF)
    block = out_refs[0].shape[0]
    for i, ref in enumerate(out_refs):
        to_core = 1 - core if i % 2 else core
        to_yl = 1 - yl if i // 2 else yl
        ref[...] = all_ref[pl.ds(pl.multiple_of((to_core * 2 + to_yl) * block, block), block)]


def finish(core, yl, total, gate, up, down, own, got, attended):
    rows = own.shape[1]
    return pl.pallas_call(
        finish_body,
        in_specs=[SM, SM, VM] + [HBM] * 6,
        out_specs=[VM] * 4,
        out_shape=[on_chip((rows // 2, DH))] * 4,
        scratch_shapes=[
            pltpu.VMEM((2 * rows, DH), BF),
            pltpu.VMEM((3, DH, DH), BF),
            pltpu.VMEM((2, rows, DH), BF),
            pltpu.VMEM((2 * rows, DH), F32),
            pltpu.SemaphoreType.DMA((6,)),
        ],
        compiler_params=PARAMS,
        cost_estimate=cost(42 * DH**3, 20 * DH * DH, rows * DH),
        name="finish",
    )(core, yl, vmem(total), *hbm(gate, up, down, own, got, attended))


def unpack_body(core_ref, yl_ref, *refs):
    out_ref = refs[4]
    core, yl = core_ref[0], yl_ref[0]
    for i, ref in enumerate(refs[:4]):
        head = 2 * (1 - yl if i // 2 else yl) + (1 - core if i % 2 else core)
        for which in range(4):

            @pl.when(head == which)
            def _():
                out_ref[:, which * DH : (which + 1) * DH] = ref[...]


def unpack(core, yl, pieces):
    rows = pieces[0].shape[0]
    return pl.pallas_call(
        unpack_body,
        in_specs=[SM, SM] + [VM] * 4,
        out_specs=VM,
        out_shape=shape((rows, 4 * DH)),
        compiler_params=PARAMS,
        cost_estimate=cost(0, 4 * rows * DH * 4),
        name="unpack",
    )(core, yl, *[vmem(p) for p in pieces])


def swap(value, axis):
    return lax.all_to_all(
        value, axis, split_axis=0, concat_axis=0, tiled=True, axis_index_groups=[ORDERS[axis]]
    )


def step(fw_q, fw_k, fw_v, fw_lr, fast_gate, fast_up, fast_down, attn_q, attn_k, attn_v):
    core = lax.axis_index("core").astype(jnp.int32).reshape(1)
    yl = lax.axis_index("yl").astype(jnp.int32).reshape(1)
    chip = lax.axis_index(CHIPS).astype(jnp.int32).reshape(1)
    pair = [(0, 1), (1, 0)]
    weights = (fast_gate, fast_up, fast_down)
    own, send = pack_grad(core, fw_k, fw_v, fw_lr)
    send, *early = lax.optimization_barrier((send,) + weights)
    partial = grads(own, lax.ppermute(send, "core", pair), pick(core, early))
    plane = lax.axis_size("plane")
    depth = lax.axis_size("z")
    partial, *rest = lax.optimization_barrier((partial, fw_q, attn_q, attn_k, attn_v))
    part = swap(partial.reshape(plane, -1, DH), "plane")
    own, send = pack_rest(core, rest)
    got = lax.ppermute(send, "core", pair)
    last = jnp.where(core == 1, own[2:, -WINDOW:], got[2:, -WINDOW:])
    part = plane_sum(part)
    part = swap(part.reshape(depth, -1, DH), "z")
    chips = lax.axis_size(CHIPS)
    halo = lax.ppermute(last, CHIPS, [(s, s + 1) for s in range(chips - 1)])
    part = sum_spread(part)
    part = swap(part, "z").reshape(-1, DH)
    spread = jnp.broadcast_to(part, (plane,) + part.shape)
    total = swap(spread, "plane").reshape(3, DH, DH)
    attended = attend(core, chip, *hbm(own, got, halo))
    kept, to_core, to_chip, to_both = finish(core, yl, total, *weights, own, got, attended)
    pieces = (
        kept,
        lax.ppermute(to_core, "core", pair),
        lax.ppermute(to_chip, "yl", pair),
        lax.ppermute(to_both, QUAD, [(s, 3 - s) for s in range(4)]),
    )
    return unpack(core, yl, pieces)


def solution(mesh):
    fine = Mesh(mesh.devices.reshape(8, 8, 2, 2), ("z", "plane", "core", "yl"))
    ctx = ("z", "plane", "core")
    wide = P(ctx, "yl")
    weight = P("yl", None, None)
    in_specs = (wide, wide, wide, wide, weight, weight, weight, wide, wide, wide)
    out_specs = P(ctx + ("yl",), None)
    return jax.shard_map(step, mesh=fine, in_specs=in_specs, out_specs=out_specs, check_vma=False)
```

profile of v0, /device:TPU:4, one launch (start us, length us, event | category | flops | bytes accessed | tf_op | source)
XLA Modules:
  0.0 116.5 jit_solution(7128641408149276613)
XLA Ops:
  0.0 1.3 %pack_grad.1 = (bf16[2,256,512]{2,1,0:T(8,128)(2,1)S(1)}, bf16[2,256,512]{2,1,0:T(8,128)(2,1)S(1)}) custom-call(s32[1]{0:T(128)} %bitcast.core_ref, bf16[256,1024]{1,0:T(8,128)(2,1)} %k_ref.1, bf16[256,1024]{1,0:T(8,128)(2,1)} %v_ref.1, f32[2,256]{1,0:T(2,128)} %bitcast.13), custom_call_target="tpu_custom_call" | custom-call | flops 262144 | bytes 2097152 | tf_op jit(solution)/shard_map/pack_grad/pallas_call | solution.py:99
  1.3 0.1 collective-permute-start
  1.4 1.4 %pick.1.weight_ref = bf16[3,512,512]{2,1,0:T(8,128)(2,1)S(1)} custom-call(s32[1]{0:T(128)} %bitcast.core_ref, bf16[2,512,512]{2,1,0:T(8,128)(2,1)} %gate_ref.2, bf16[2,512,512]{2,1,0:T(8,128)(2,1)} %up_ref.2, bf16[2,512,512]{2,1,0:T(8,128)(2,1)} %down_ref.2), custom_call_target="tpu_custom_call" | custom-call | bytes 1572864 | tf_op jit(solution)/shard_map/pick/pallas_call | solution.py:121
  2.8 0.5 collective-permute-done.got_ref
  3.3 2.3 %grads.1 = bf16[3,512,512]{2,1,0:T(8,128)(2,1)S(1)} custom-call(bf16[2,256,512]{2,1,0:T(8,128)(2,1)S(1)} %get-tuple-element.22.own_ref, bf16[2,256,512]{2,1,0:T(8,128)(2,1)S(1)} %collective-permute-done.got_ref, bf16[3,512,512]{2,1,0:T(8,128)(2,1)S(1)} %pick.1.weight_ref), custom_call_target="tpu_custom_call" | custom-call | flops 1610612736 | bytes 4194304 | tf_op jit(solution)/shard_map/grads/pallas_call | solution.py:177
  5.6 27.9 %all_to_all.20.in_ref = bf16[8,192,512]{2,1,0:T(8,128)(2,1)S(1)} all-to-all(bf16[8,192,512]{2,1,0:T(8,128)(2,1)S(1)} %bitcast.10), channel_id=1, replica_groups={{0,20,8,28,16,4,24,12},{1,21,9,29,17,5,25,13},{2,22,10,30,18,6,26,14},{..., dimensions={0} | all-to-all | bytes 3145728 | tf_op jit(solution)/shard_map/all_to_all | solution.py:378
  33.5 0.2 plane_sum.1
  33.7 16.3 %all_to_all.21.in_ref = bf16[8,24,512]{2,1,0:T(8,128)(2,1)S(1)} all-to-all(bf16[8,24,512]{2,1,0:T(8,128)(2,1)S(1)} %bitcast.11), channel_id=1, replica_groups={{0,64,128,192,32,96,160,224},{1,65,129,193,33,97,161,225},{2,66,130,194..., dimensions={0} | all-to-all | bytes 393216 | tf_op jit(solution)/shard_map/all_to_all | solution.py:378
  50.0 0.7 depth_sum.1
  50.7 3.6 %all-to-all-start.2 = ((bf16[8,24,512]{2,1,0:T(8,128)(2,1)}), bf16[8,24,512]{2,1,0:T(8,128)(2,1)S(1)}, u32[]{:S(2)}, u32[]{:S(2)}) async-start(bf16[8,24,512]{2,1,0:T(8,128)(2,1)} %depth_sum.1), calls=%async_computation.2 | async-start | bytes 393216 | tf_op jit(solution)/shard_map/all_to_all | solution.py:378
  54.3 2.6 %pack_rest.1 = (bf16[4,256,512]{2,1,0:T(8,128)(2,1)S(1)}, bf16[4,256,512]{2,1,0:T(8,128)(2,1)}) custom-call(s32[1]{0:T(128)} %bitcast.core_ref, bf16[256,1024]{1,0:T(8,128)(2,1)} %refs_0_, bf16[256,1024]{1,0:T(8,128)(2,1)} %refs_1_, bf16[256,1024]{1,0:T(8,128)(2,1)} %refs_2_, bf16[256,1024]{1,0:T(8,128)(2,1)} %refs_3_), custom_call_target="tpu_custom_call" | custom-call | bytes 4194304 | tf_op jit(solution)/shard_map/pack_rest/pallas_call | solution.py:144
  56.8 0.0 copy-start
  56.9 0.1 collective-permute-start.1
  57.0 5.4 %all-to-all-done.2 = bf16[8,24,512]{2,1,0:T(8,128)(2,1)S(1)} async-done(((bf16[8,24,512]{2,1,0:T(8,128)(2,1)}), bf16[8,24,512]{2,1,0:T(8,128)(2,1)S(1)}, u32[]{:S(2)}, u32[]{:S(2)}) %all-to-all-start.2) | async-done | bytes 196640 | tf_op jit(solution)/shard_map/all_to_all | solution.py:378
  62.4 1.3 %broadcast_in_dim.11 = bf16[8,192,512]{2,1,0:T(8,128)(2,1)} broadcast(bf16[192,512]{1,0:T(8,128)(2,1)S(1)} %bitcast.12), dimensions={1,2} | broadcast | bytes 1769472 | tf_op jit(solution)/shard_map/broadcast_in_dim | solution.py:405
  63.7 6.2 %all-to-all-start.3 = ((bf16[8,192,512]{2,1,0:T(8,128)(2,1)}), bf16[8,192,512]{2,1,0:T(8,128)(2,1)S(1)}, u32[]{:S(2)}, u32[]{:S(2)}) async-start(bf16[8,192,512]{2,1,0:T(8,128)(2,1)} %broadcast_in_dim.11), calls=%async_computation.3 | async-start | bytes 3145728 | tf_op jit(solution)/shard_map/all_to_all | solution.py:378
  69.8 0.0 collective-permute-done.1.got_ref
  69.8 0.0 copy-done
  69.8 1.0 slice_select_fusion
  70.8 4.9 %collective-permute-start.2 = (bf16[2,128,512]{2,1,0:T(8,128)(2,1)S(1)}, bf16[2,128,512]{2,1,0:T(8,128)(2,1)S(1)}, u32[]{:S(2)}, u32[]{:S(2)}) collective-permute-start(bf16[2,128,512]{2,1,0:T(8,128)(2,1)S(1)} %slice_select_fusion), channel_id=1, source_target_pairs={{0,4},{4,8},{8,12},{12,16},{16,20},{20,24},{24,28},{28,32},{32,36}... | collective-permute-start | bytes 786440 | tf_op jit(solution)/shard_map/ppermute | solution.py:402
  75.7 19.4 %collective-permute-done.2.halo_ref = bf16[2,128,512]{2,1,0:T(8,128)(2,1)S(1)} collective-permute-done((bf16[2,128,512]{2,1,0:T(8,128)(2,1)S(1)}, bf16[2,128,512]{2,1,0:T(8,128)(2,1)S(1)}, u32[]{:S(2)}, u32[]{:S(2)}) %collective-permute-start.2) | collective-permute-done | bytes 262176 | tf_op jit(solution)/shard_map/ppermute | solution.py:402
  95.1 0.0 copy-start.1
  95.1 0.7 copy-done.1
  95.8 4.1 %window_attention.1.att_ref = f32[512,512]{1,0:T(8,128)} custom-call(s32[1]{0:T(128)} %bitcast.core_ref, s32[1]{0:T(128)} %bitcast.7.chip_ref, bf16[4,256,512]{2,1,0:T(8,128)(2,1)} %copy-done, bf16[4,256,512]{2,1,0:T(8,128)(2,1)} %collective-permute-done.1.got_ref, bf16[2,128,512]{2,1,0:T(8,128)(2,1)} %copy-done.1), custom_call_target="tpu_custom_call" | custom-call | flops 268435456 | bytes 1572864 | tf_op jit(solution)/shard_map/window_attention/pallas_call | solution.py:265
  99.9 0.0 all-to-all-done.3
  100.0 7.4 %finish.1 = (bf16[128,512]{1,0:T(8,128)(2,1)S(1)}, bf16[128,512]{1,0:T(8,128)(2,1)S(1)}, bf16[128,512]{1,0:T(8,128)(2,1)S(1)}, bf16[128,512]{1,0:T(8,128)(2,1)S(1)}) custom-call(s32[1]{0:T(128)} %bitcast.core_ref, s32[1]{0:T(128)} %bitcast.1.yl_ref, bf16[3,512,512]{2,1,0:T(8,128)(2,1)S(1)} %bitcast.9, bf16[2,512,512]{2,1,0:T(8,128)(2,1)} %gate_ref.2, ...), custom_call_target="tpu_custom_call" | custom-call | flops 5637144576 | bytes 5242880 | tf_op jit(solution)/shard_map/finish/pallas_call | solution.py:334
  107.4 0.1 collective-permute-start.3
  107.5 0.8 collective-permute-start.4
  108.3 1.1 collective-permute-start.5
  109.3 0.0 collective-permute-done.3.refs_1_
  109.3 4.6 %collective-permute-done.4.refs_2_ = bf16[128,512]{1,0:T(8,128)(2,1)S(1)} collective-permute-done((bf16[128,512]{1,0:T(8,128)(2,1)S(1)}, bf16[128,512]{1,0:T(8,128)(2,1)S(1)}, u32[]{:S(2)}, u32[]{:S(2)}) %collective-permute-start.4) | collective-permute-done | bytes 131104 | tf_op jit(solution)/shard_map/ppermute | solution.py:412
  114.0 1.7 %collective-permute-done.5.refs_3_ = bf16[128,512]{1,0:T(8,128)(2,1)S(1)} collective-permute-done((bf16[128,512]{1,0:T(8,128)(2,1)S(1)}, bf16[128,512]{1,0:T(8,128)(2,1)S(1)}, u32[]{:S(2)}, u32[]{:S(2)}) %collective-permute-start.5) | collective-permute-done | bytes 131104 | tf_op jit(solution)/shard_map/ppermute | solution.py:413
  115.6 0.9 unpack.1
Async XLA Ops:
  1.3 2.0 %collective-permute-start = (bf16[2,256,512]{2,1,0:T(8,128)(2,1)S(1)}, bf16[2,256,512]{2,1,0:T(8,128)(2,1)S(1)}, u32[]{:S(2)}, u32[]{:S(2)}) collective-permute-start(bf16[2,256,512]{2,1,0:T(8,128)(2,1)S(1)} %get-tuple-element.24), channel_id=1, source_target_pairs={{0,2},{2,0},{1,3},{3,1},{4,6},{6,4},{5,7},{7,5},{8,10},{10,8},{9,1... | collective-permute-start | bytes 1572872 | tf_op jit(solution)/shard_map/ppermute | solution.py:391
  50.7 11.7 %all-to-all-start.2 = ((bf16[8,24,512]{2,1,0:T(8,128)(2,1)}), bf16[8,24,512]{2,1,0:T(8,128)(2,1)S(1)}, u32[]{:S(2)}, u32[]{:S(2)}) async-start(bf16[8,24,512]{2,1,0:T(8,128)(2,1)} %depth_sum.1), calls=%async_computation.2 | async-start | bytes 393216 | tf_op jit(solution)/shard_map/all_to_all | solution.py:378
  56.8 13.0 %copy-start = (bf16[4,256,512]{2,1,0:T(8,128)(2,1)}, bf16[4,256,512]{2,1,0:T(8,128)(2,1)S(1)}, u32[]{:S(2)}) copy-start(bf16[4,256,512]{2,1,0:T(8,128)(2,1)S(1)} %get-tuple-element.33.own_ref) | copy-start | bytes 3145732
  56.9 13.0 %collective-permute-start.1 = (bf16[4,256,512]{2,1,0:T(8,128)(2,1)}, bf16[4,256,512]{2,1,0:T(8,128)(2,1)}, u32[]{:S(2)}, u32[]{:S(2)}) collective-permute-start(bf16[4,256,512]{2,1,0:T(8,128)(2,1)} %get-tuple-element.34), channel_id=1, source_target_pairs={{0,2},{2,0},{1,3},{3,1},{4,6},{6,4},{5,7},{7,5},{8,10},{10,8},{9,1... | collective-permute-start | bytes 3145736 | tf_op jit(solution)/shard_map/ppermute | solution.py:397
  63.7 36.3 %all-to-all-start.3 = ((bf16[8,192,512]{2,1,0:T(8,128)(2,1)}), bf16[8,192,512]{2,1,0:T(8,128)(2,1)S(1)}, u32[]{:S(2)}, u32[]{:S(2)}) async-start(bf16[8,192,512]{2,1,0:T(8,128)(2,1)} %broadcast_in_dim.11), calls=%async_computation.3 | async-start | bytes 3145728 | tf_op jit(solution)/shard_map/all_to_all | solution.py:378
  70.8 24.3 %collective-permute-start.2 = (bf16[2,128,512]{2,1,0:T(8,128)(2,1)S(1)}, bf16[2,128,512]{2,1,0:T(8,128)(2,1)S(1)}, u32[]{:S(2)}, u32[]{:S(2)}) collective-permute-start(bf16[2,128,512]{2,1,0:T(8,128)(2,1)S(1)} %slice_select_fusion), channel_id=1, source_target_pairs={{0,4},{4,8},{8,12},{12,16},{16,20},{20,24},{24,28},{28,32},{32,36}... | collective-permute-start | bytes 786440 | tf_op jit(solution)/shard_map/ppermute | solution.py:402
  95.1 0.7 copy-start.1
  107.4 2.0 %collective-permute-start.3 = (bf16[128,512]{1,0:T(8,128)(2,1)S(1)}, bf16[128,512]{1,0:T(8,128)(2,1)S(1)}, u32[]{:S(2)}, u32[]{:S(2)}) collective-permute-start(bf16[128,512]{1,0:T(8,128)(2,1)S(1)} %get-tuple-element.36), channel_id=1, source_target_pairs={{0,2},{2,0},{1,3},{3,1},{4,6},{6,4},{5,7},{7,5},{8,10},{10,8},{9,1... | collective-permute-start | bytes 393224 | tf_op jit(solution)/shard_map/ppermute | solution.py:411
  107.5 6.5 %collective-permute-start.4 = (bf16[128,512]{1,0:T(8,128)(2,1)S(1)}, bf16[128,512]{1,0:T(8,128)(2,1)S(1)}, u32[]{:S(2)}, u32[]{:S(2)}) collective-permute-start(bf16[128,512]{1,0:T(8,128)(2,1)S(1)} %get-tuple-element.37), channel_id=1, source_target_pairs={{0,1},{1,0},{2,3},{3,2},{4,5},{5,4},{6,7},{7,6},{8,9},{9,8},{10,11... | collective-permute-start | bytes 393224 | tf_op jit(solution)/shard_map/ppermute | solution.py:412
  108.3 7.4 %collective-permute-start.5 = (bf16[128,512]{1,0:T(8,128)(2,1)S(1)}, bf16[128,512]{1,0:T(8,128)(2,1)S(1)}, u32[]{:S(2)}, u32[]{:S(2)}) collective-permute-start(bf16[128,512]{1,0:T(8,128)(2,1)S(1)} %get-tuple-element.38), channel_id=1, source_target_pairs={{0,3},{1,2},{2,1},{3,0},{4,7},{5,6},{6,5},{7,4},{8,11},{9,10},{10,... | collective-permute-start | bytes 393224 | tf_op jit(solution)/shard_map/ppermute | solution.py:413
where the time goes:
time: 118 us; the launch traced here: 117 us
  blocking collectives  44.2 us (37%)
  waiting for transfers between devices  31.6 us (27%)
  Pallas kernels  20.8 us (18%)
  starting transfers between devices  16.7 us (14%)
  local copies, waits for them, and re-layouts  2.01 us (2%)
    all_to_all x2, blocking collectives, swap(): lax.all_to_all(value, axis, split_axis=0, concat_axis=0, tiled=True, axis...  44.2 us
    ppermute x1, waiting for transfers between devices, step(): halo = lax.ppermute(last, CHIPS, [(s, s + 1) for s in range(chips - 1)])  19.4 us
    all_to_all x2, starting transfers between devices, swap(): lax.all_to_all(value, axis, split_axis=0, concat_axis=0, tiled=True, axis...  9.74 us
    pallas_call x1, Pallas kernels, finish(): pl.pallas_call(finish_body, in_specs=[SM, SM, VM] + [HBM] * 6, out_specs=...  7.43 us
    all_to_all x2, waiting for transfers between devices, swap(): lax.all_to_all(value, axis, split_axis=0, concat_axis=0, tiled=True, axis...  5.41 us
    ppermute x1, starting transfers between devices, step(): halo = lax.ppermute(last, CHIPS, [(s, s + 1) for s in range(chips - 1)])  4.85 us
    ppermute x1, waiting for transfers between devices, step(): lax.ppermute(to_chip, 'yl', pair)  4.61 us
    pallas_call x1, Pallas kernels, attend(): pl.pallas_call(attend_body, in_specs=[SM, SM, HBM, HBM, HBM], out_specs=H...  4.12 us
  transfers between devices with their start and end apart: 8, of which 5 were waited for; matrix products, arithmetic and copies ran while one was open for 2% of the time, Pallas kernels for 7%

commit v1 on v0

--- a/solution.py
+++ b/solution.py
@@ -60,6 +60,11 @@
 HBM = pl.BlockSpec(memory_space=pltpu.HBM)
 
 
+def seat(place_ref):
+    place = place_ref[0]
+    return (place >> 1) & 1, place & 1, place >> 2
+
+
 def half(ref, which):
     return ref.at[:, pl.ds(pl.multiple_of(which * DH, DH), DH)]
 
@@ -76,8 +81,8 @@
         copy.wait()
 
 
-def pack_grad_body(core_ref, k_ref, v_ref, lr_ref, own_ref, send_ref, value_ref, rate_ref, sems):
-    core = core_ref[0]
+def pack_grad_body(place_ref, k_ref, v_ref, lr_ref, own_ref, send_ref, value_ref, rate_ref, sems):
+    core, _, _ = seat(place_ref)
     rows = k_ref.shape[0]
     sides = ((send_ref, 1 - core), (own_ref, core))
     pairs = [(half(v_ref, which), value_ref.at[i]) for i, (_, which) in enumerate(sides)]
@@ -94,7 +99,7 @@
     wait_all(copies[3:])
 
 
-def pack_grad(core, fw_k, fw_v, fw_lr):
+def pack_grad(place, fw_k, fw_v, fw_lr):
     rows = fw_k.shape[0]
     return pl.pallas_call(
         pack_grad_body,
@@ -109,48 +114,29 @@
         compiler_params=PARAMS,
         cost_estimate=cost(rows * 1024, 8 * rows * 1024),
         name="pack_grad",
-    )(core, *hbm(fw_k, fw_v, fw_lr.T))
-
-
-def pick_body(core_ref, gate_ref, up_ref, down_ref, out_ref, sems):
-    pairs = [(w.at[core_ref[0]], out_ref.at[i]) for i, w in enumerate((gate_ref, up_ref, down_ref))]
+    )(place, *hbm(fw_k, fw_v, fw_lr.T))
+
+
+def pick_body(place_ref, *refs):
+    out_ref, send_ref, sems = refs[7:]
+    core, _, _ = seat(place_ref)
+    pairs = [(half(source, 1 - core), send_ref.at[i]) for i, source in enumerate(refs[3:7])]
+    pairs += [(w.at[core], out_ref.at[i]) for i, w in enumerate(refs[:3])]
     wait_all(start_all(pairs, sems))
 
 
-def pick(core, weights):
+def pick(place, weights, arrays):
+    rows = arrays[0].shape[0]
     return pl.pallas_call(
         pick_body,
-        in_specs=[SM] + [HBM] * 3,
-        out_specs=VM,
-        out_shape=on_chip((3, DH, DH)),
-        scratch_shapes=[pltpu.SemaphoreType.DMA((3,))],
-        compiler_params=PARAMS,
-        cost_estimate=cost(0, 6 * DH * DH),
+        in_specs=[SM] + [HBM] * 7,
+        out_specs=[VM, VM],
+        out_shape=[on_chip((3, DH, DH)), on_chip((4, rows, DH))],
+        scratch_shapes=[pltpu.SemaphoreType.DMA((7,))],
+        compiler_params=PARAMS,
+        cost_estimate=cost(0, 6 * DH * DH + 8 * rows * DH),
         name="pick",
-    )(core, *hbm(*weights))
-
-
-def pack_rest_body(core_ref, *refs):
-    own_ref, send_ref, sems = refs[4:]
-    core = core_ref[0]
-    pairs = []
-    for ref, which in ((send_ref, 1 - core), (own_ref, core)):
-        pairs += [(half(source, which), ref.at[i]) for i, source in enumerate(refs[:4])]
-    wait_all(start_all(pairs, sems))
-
-
-def pack_rest(core, arrays):
-    rows = arrays[0].shape[0]
-    return pl.pallas_call(
-        pack_rest_body,
-        in_specs=[SM] + [HBM] * 4,
-        out_specs=[VM, VM],
-        out_shape=[shape((4, rows, DH)), shape((4, rows, DH))],
-        scratch_shapes=[pltpu.SemaphoreType.DMA((8,))],
-        compiler_params=PARAMS,
-        cost_estimate=cost(0, 16 * rows * 1024),
-        name="pack_rest",
-    )(core, *hbm(*arrays))
+    )(place, *hbm(*weights, *arrays))
 
 
 def grads_body(own_ref, got_ref, weight_ref, out_ref):
@@ -178,7 +164,7 @@
         grads_body,
         in_specs=[VM] * 3,
         out_specs=VM,
-        out_shape=shape((3, DH, DH)),
+        out_shape=on_chip((3, DH, DH)),
         compiler_params=PARAMS,
         cost_estimate=cost(12 * tokens * DH * DH, 8 * DH * DH * 2, tokens * DH),
         name="grads",
@@ -210,6 +196,28 @@
     )(vmem(parts))
 
 
+def tail_body(place_ref, k_ref, v_ref, got_ref, out_ref, sems):
+    core, _, _ = seat(place_ref)
+    tail = pl.ds(k_ref.shape[0] - WINDOW, WINDOW)
+    kept = [(half(ref, 1).at[tail], out_ref.at[i]) for i, ref in enumerate((k_ref, v_ref))]
+    other = [(got_ref.at[2 + i, tail], out_ref.at[i]) for i in range(2)]
+    pl.when(core == 1)(lambda: wait_all(start_all(kept, sems)))
+    pl.when(core != 1)(lambda: wait_all(start_all(other, sems)))
+
+
+def last_rows(place, attn_k, attn_v, got):
+    return pl.pallas_call(
+        tail_body,
+        in_specs=[SM, HBM, HBM, HBM],
+        out_specs=VM,
+        out_shape=on_chip((2, WINDOW, DH)),
+        scratch_shapes=[pltpu.SemaphoreType.DMA((2,))],
+        compiler_params=PARAMS,
+        cost_estimate=cost(0, 8 * WINDOW * DH),
+        name="tail",
+    )(place, *hbm(attn_k, attn_v, got))
+
+
 def sum_spread_body(in_ref, out_ref):
     total = add_up(in_ref, slice(None))
     for i in range(out_ref.shape[0]):
@@ -228,21 +236,23 @@
     )(vmem(parts))
 
 
-def attend_body(core_ref, chip_ref, own_ref, got_ref, halo_ref, out_ref, *scratch):
+def attend_body(place_ref, own_q, own_k, own_v, got_ref, halo_ref, out_ref, *scratch):
     q_ref, k_ref, v_ref, result_ref, sems, out_sem = scratch
-    rows = own_ref.shape[1]
+    core, _, chip = seat(place_ref)
+    rows = own_q.shape[0]
     pairs = [(halo_ref.at[0], k_ref.at[:WINDOW]), (halo_ref.at[1], v_ref.at[:WINDOW])]
-    for source, which in ((own_ref, core_ref[0]), (got_ref, 1 - core_ref[0])):
+    own = [half(ref, core) for ref in (own_q, own_k, own_v)]
+    for sources, which in ((own, core), ([got_ref.at[i] for i in (1, 2, 3)], 1 - core)):
         start = pl.multiple_of(which * rows, rows)
-        pairs.append((source.at[1], q_ref.at[pl.ds(start, rows)]))
-        pairs.append((source.at[2], k_ref.at[pl.ds(start + WINDOW, rows)]))
-        pairs.append((source.at[3], v_ref.at[pl.ds(start + WINDOW, rows)]))
+        pairs.append((sources[0], q_ref.at[pl.ds(start, rows)]))
+        pairs.append((sources[1], k_ref.at[pl.ds(start + WINDOW, rows)]))
+        pairs.append((sources[2], v_ref.at[pl.ds(start + WINDOW, rows)]))
     wait_all(start_all(pairs, sems))
     scale = 1.0 / math.sqrt(SWA_DH)
     row = lax.broadcasted_iota(jnp.int32, (WINDOW, 2 * WINDOW), 0)
     col = lax.broadcasted_iota(jnp.int32, (WINDOW, 2 * WINDOW), 1)
     inside = (col > row) & (col <= row + WINDOW)
-    first = inside & ((col >= WINDOW) | (chip_ref[0] > 0))
+    first = inside & ((col >= WINDOW) | (chip > 0))
     for b in range(2 * rows // WINDOW):
         seen = first if b == 0 else inside
         queries = slice(b * WINDOW, (b + 1) * WINDOW)
@@ -260,11 +270,11 @@
     copy.wait()
 
 
-def attend(core, chip, own, got, halo):
-    rows = own.shape[1]
+def attend(place, own, got, halo):
+    rows = got.shape[1]
     return pl.pallas_call(
         attend_body,
-        in_specs=[SM, SM, HBM, HBM, HBM],
+        in_specs=[SM, HBM, HBM, HBM, HBM, VM],
         out_specs=HBM,
         out_shape=pltpu.HBM((2 * rows, DH), F32),
         scratch_shapes=[
@@ -278,7 +288,7 @@
         compiler_params=PARAMS,
         cost_estimate=cost(2 * rows * 8 * WINDOW * DH, 12 * rows * DH, 4 * rows * DH),
         name="window_attention",
-    )(core, chip, *hbm(own, got, halo))
+    )(place, *hbm(*own, got), vmem(halo))
 
 
 def refresh(weight, update):
@@ -290,14 +300,14 @@
 
 
 def finish_body(
-    core_ref, yl_ref, sum_ref, gate_ref, up_ref, down_ref, own_ref, got_ref, att_ref, *rest
+    place_ref, sum_ref, gate_ref, up_ref, down_ref, own_ref, got_ref, att_ref, *rest
 ):
     out_refs = rest[:4]
     all_ref, weight_ref, query_ref, attended_ref, sems = rest[4:]
-    core, yl = core_ref[0], yl_ref[0]
-    rows = own_ref.shape[1]
+    core, yl, _ = seat(place_ref)
+    rows = own_ref.shape[0]
     pairs = [(w.at[core], weight_ref.at[i]) for i, w in enumerate((gate_ref, up_ref, down_ref))]
-    pairs += [(own_ref.at[0], query_ref.at[0]), (got_ref.at[0], query_ref.at[1])]
+    pairs += [(half(own_ref, core), query_ref.at[0]), (got_ref.at[0], query_ref.at[1])]
     copies = start_all(pairs + [(att_ref, attended_ref)], sems)
     iterates = []
     for m in range(3):
@@ -329,11 +339,11 @@
         ref[...] = all_ref[pl.ds(pl.multiple_of((to_core * 2 + to_yl) * block, block), block)]
 
 
-def finish(core, yl, total, gate, up, down, own, got, attended):
-    rows = own.shape[1]
+def finish(place, total, gate, up, down, own, got, attended):
+    rows = own.shape[0]
     return pl.pallas_call(
         finish_body,
-        in_specs=[SM, SM, VM] + [HBM] * 6,
+        in_specs=[SM, VM] + [HBM] * 6,
         out_specs=[VM] * 4,
         out_shape=[on_chip((rows // 2, DH))] * 4,
         scratch_shapes=[
@@ -346,12 +356,12 @@
         compiler_params=PARAMS,
         cost_estimate=cost(42 * DH**3, 20 * DH * DH, rows * DH),
         name="finish",
-    )(core, yl, vmem(total), *hbm(gate, up, down, own, got, attended))
-
-
-def unpack_body(core_ref, yl_ref, *refs):
+    )(place, vmem(total), *hbm(gate, up, down, own, got, attended))
+
+
+def unpack_body(place_ref, *refs):
     out_ref = refs[4]
-    core, yl = core_ref[0], yl_ref[0]
+    core, yl, _ = seat(place_ref)
     for i, ref in enumerate(refs[:4]):
         head = 2 * (1 - yl if i // 2 else yl) + (1 - core if i % 2 else core)
         for which in range(4):
@@ -361,17 +371,17 @@
                 out_ref[:, which * DH : (which + 1) * DH] = ref[...]
 
 
-def unpack(core, yl, pieces):
+def unpack(place, pieces):
     rows = pieces[0].shape[0]
     return pl.pallas_call(
         unpack_body,
-        in_specs=[SM, SM] + [VM] * 4,
+        in_specs=[SM] + [VM] * 4,
         out_specs=VM,
         out_shape=shape((rows, 4 * DH)),
         compiler_params=PARAMS,
         cost_estimate=cost(0, 4 * rows * DH * 4),
         name="unpack",
-    )(core, yl, *[vmem(p) for p in pieces])
+    )(place, *[vmem(p) for p in pieces])
 
 
 def swap(value, axis):
@@ -381,38 +391,35 @@
 
 
 def step(fw_q, fw_k, fw_v, fw_lr, fast_gate, fast_up, fast_down, attn_q, attn_k, attn_v):
-    core = lax.axis_index("core").astype(jnp.int32).reshape(1)
-    yl = lax.axis_index("yl").astype(jnp.int32).reshape(1)
-    chip = lax.axis_index(CHIPS).astype(jnp.int32).reshape(1)
+    place = lax.axis_index(CHIPS + QUAD).astype(jnp.int32).reshape(1)
     pair = [(0, 1), (1, 0)]
     weights = (fast_gate, fast_up, fast_down)
-    own, send = pack_grad(core, fw_k, fw_v, fw_lr)
+    rest = (fw_q, attn_q, attn_k, attn_v)
+    own, send = pack_grad(place, fw_k, fw_v, fw_lr)
     send, *early = lax.optimization_barrier((send,) + weights)
-    partial = grads(own, lax.ppermute(send, "core", pair), pick(core, early))
+    moved = lax.ppermute(send, "core", pair)
+    picked, send = pick(place, early, rest)
+    got = lax.ppermute(send, "core", pair)
+    partial = grads(own, moved, picked)
     plane = lax.axis_size("plane")
     depth = lax.axis_size("z")
-    partial, *rest = lax.optimization_barrier((partial, fw_q, attn_q, attn_k, attn_v))
     part = swap(partial.reshape(plane, -1, DH), "plane")
-    own, send = pack_rest(core, rest)
-    got = lax.ppermute(send, "core", pair)
-    last = jnp.where(core == 1, own[2:, -WINDOW:], got[2:, -WINDOW:])
     part = plane_sum(part)
     part = swap(part.reshape(depth, -1, DH), "z")
+    last = last_rows(place, attn_k, attn_v, got)
     chips = lax.axis_size(CHIPS)
     halo = lax.ppermute(last, CHIPS, [(s, s + 1) for s in range(chips - 1)])
     part = sum_spread(part)
     part = swap(part, "z").reshape(-1, DH)
     spread = jnp.broadcast_to(part, (plane,) + part.shape)
     total = swap(spread, "plane").reshape(3, DH, DH)
-    attended = attend(core, chip, *hbm(own, got, halo))
-    kept, to_core, to_chip, to_both = finish(core, yl, total, *weights, own, got, attended)
-    pieces = (
-        kept,
-        lax.ppermute(to_core, "core", pair),
-        lax.ppermute(to_chip, "yl", pair),
-        lax.ppermute(to_both, QUAD, [(s, 3 - s) for s in range(4)]),
-    )
-    return unpack(core, yl, pieces)
+    attended = attend(place, rest[1:], got, halo)
+    kept, to_core, to_chip, to_both = finish(place, total, *weights, fw_q, got, attended)
+    from_chip = lax.ppermute(to_chip, "yl", pair)
+    from_both = lax.ppermute(to_both, QUAD, [(s, 3 - s) for s in range(4)])
+    from_core = lax.ppermute(to_core, "core", pair)
+    pieces = (kept, from_core, from_chip, from_both)
+    return unpack(place, pieces)
 
 
 def solution(mesh):

time: 118 us -> 116 us (0.983)
  blocking collectives: 44.2 us -> 56.3 us
  waiting for transfers between devices: 31.6 us -> 24.5 us
  starting transfers between devices: 16.7 us -> 12.1 us
  Pallas kernels: 20.8 us -> 19.1 us
    all_to_all x2 -> x3, blocking collectives: 44.2 us -> 56.3 us  [swap(): lax.all_to_all(value, axis, split_axis=0, concat_axis=0, tiled=True, axis...]
    all_to_all x2 -> x1, waiting for transfers between devices: 5.41 us -> 0.01 us  [swap(): lax.all_to_all(value, axis, split_axis=0, concat_axis=0, tiled=True, axis...]
    all_to_all x2 -> x1, starting transfers between devices: 9.74 us -> 5.2 us  [swap(): lax.all_to_all(value, axis, split_axis=0, concat_axis=0, tiled=True, axis...]
    ppermute x1, waiting for transfers between devices: 19.4 us -> 15.4 us  [step(): halo = lax.ppermute(last, CHIPS, [(s, s + 1) for s in range(chips - 1)])]
    ppermute x1, waiting for transfers between devices: 0.01 us -> 2.66 us  [step(): got = lax.ppermute(send, 'core', pair)]
  transfers between devices with their start and end apart: 8 -> 7, of which waited for: 5 -> 5; matrix products, arithmetic and copies ran while one was open for 2% -> 0% of each run, Pallas kernels for 7% -> 6%
where the time goes in v1:
time: 116 us; the launch traced here: 114 us
  blocking collectives  56.3 us (49%)
  waiting for transfers between devices  24.5 us (21%)
  Pallas kernels  19.1 us (16%)
  starting transfers between devices  12.1 us (10%)
  local copies, waits for them, and re-layouts  2.26 us (2%)
    all_to_all x3, blocking collectives, swap(): lax.all_to_all(value, axis, split_axis=0, concat_axis=0, tiled=True, axis...  56.3 us
    ppermute x1, waiting for transfers between devices, step(): halo = lax.ppermute(last, CHIPS, [(s, s + 1) for s in range(chips - 1)])  15.4 us
    pallas_call x1, Pallas kernels, finish(): pl.pallas_call(finish_body, in_specs=[SM, VM] + [HBM] * 6, out_specs=[VM]...  7.43 us
    all_to_all x1, starting transfers between devices, swap(): lax.all_to_all(value, axis, split_axis=0, concat_axis=0, tiled=True, axis...  5.2 us
    ppermute x1, starting transfers between devices, step(): halo = lax.ppermute(last, CHIPS, [(s, s + 1) for s in range(chips - 1)])  4.87 us
    ppermute x1, waiting for transfers between devices, step(): from_chip = lax.ppermute(to_chip, 'yl', pair)  4.61 us
    pallas_call x1, Pallas kernels, attend(): pl.pallas_call(attend_body, in_specs=[SM, HBM, HBM, HBM, HBM, VM], out_sp...  4.31 us
    ppermute x1, waiting for transfers between devices, step(): got = lax.ppermute(send, 'core', pair)  2.66 us
  transfers between devices with their start and end apart: 7, of which 5 were waited for; matrix products, arithmetic and copies ran while one was open for 0% of the time, Pallas kernels for 6%

profile of v1, /device:TPU:4, one launch (start us, length us, event | category | flops | bytes accessed | tf_op | source)
XLA Modules:
  0.0 114.4 jit_solution(16746623789001926253)
XLA Ops:
  0.0 1.3 %pack_grad.1 = (bf16[2,256,512]{2,1,0:T(8,128)(2,1)S(1)}, bf16[2,256,512]{2,1,0:T(8,128)(2,1)S(1)}) custom-call(s32[1]{0:T(128)} %bitcast.place_ref, bf16[256,1024]{1,0:T(8,128)(2,1)} %k_ref.2, bf16[256,1024]{1,0:T(8,128)(2,1)} %v_ref.2, f32[2,256]{1,0:T(2,128)} %bitcast.10), custom_call_target="tpu_custom_call" | custom-call | flops 262144 | bytes 2097152 | tf_op jit(solution)/shard_map/pack_grad/pallas_call | solution.py:104
  1.3 0.1 collective-permute-start
  1.4 1.7 %pick.1 = (bf16[3,512,512]{2,1,0:T(8,128)(2,1)S(1)}, bf16[4,256,512]{2,1,0:T(8,128)(2,1)S(1)}) custom-call(s32[1]{0:T(128)} %bitcast.place_ref, bf16[2,512,512]{2,1,0:T(8,128)(2,1)} %gate_ref.1, bf16[2,512,512]{2,1,0:T(8,128)(2,1)} %up_ref.1, bf16[2,512,512]{2,1,0:T(8,128)(2,1)} %down_ref.1, bf16[256,1024]{1,0:T(8,128)(2,1)} %own_ref.1, ...), custom_call_target="tpu_custom_call" | custom-call | bytes 2621440 | tf_op jit(solution)/shard_map/pick/pallas_call | solution.py:130
  3.1 0.1 collective-permute-done.got_ref
  3.3 2.3 %grads.1 = bf16[3,512,512]{2,1,0:T(8,128)(2,1)S(1)} custom-call(bf16[2,256,512]{2,1,0:T(8,128)(2,1)S(1)} %get-tuple-element.17.own_ref, bf16[2,256,512]{2,1,0:T(8,128)(2,1)S(1)} %collective-permute-done.got_ref, bf16[3,512,512]{2,1,0:T(8,128)(2,1)S(1)} %get-tuple-element.23.weight_ref), custom_call_target="tpu_custom_call" | custom-call | flops 1610612736 | bytes 4194304 | tf_op jit(solution)/shard_map/grads/pallas_call | solution.py:163
  5.6 28.1 %all_to_all.20.in_ref = bf16[8,192,512]{2,1,0:T(8,128)(2,1)S(1)} all-to-all(bf16[8,192,512]{2,1,0:T(8,128)(2,1)S(1)} %bitcast.7), channel_id=1, replica_groups={{0,20,8,28,16,4,24,12},{1,21,9,29,17,5,25,13},{2,22,10,30,18,6,26,14},{..., dimensions={0} | all-to-all | bytes 3145728 | tf_op jit(solution)/shard_map/all_to_all | solution.py:388
  33.7 0.2 plane_sum.1
  33.9 16.3 %all_to_all.21.in_ref = bf16[8,24,512]{2,1,0:T(8,128)(2,1)S(1)} all-to-all(bf16[8,24,512]{2,1,0:T(8,128)(2,1)S(1)} %bitcast.8), channel_id=1, replica_groups={{0,64,128,192,32,96,160,224},{1,65,129,193,33,97,161,225},{2,66,130,194..., dimensions={0} | all-to-all | bytes 393216 | tf_op jit(solution)/shard_map/all_to_all | solution.py:388
  50.3 11.8 %all_to_all.22 = bf16[8,24,512]{2,1,0:T(8,128)(2,1)S(1)} all-to-all(bf16[8,24,512]{2,1,0:T(8,128)(2,1)S(1)} %depth_sum.1), channel_id=1, replica_groups={{0,64,128,192,32,96,160,224},{1,65,129,193,33,97,161,225},{2,66,130,194..., dimensions={0} | all-to-all | bytes 393216 | tf_op jit(solution)/shard_map/all_to_all | solution.py:388
  62.1 1.3 %broadcast_in_dim.3 = bf16[8,192,512]{2,1,0:T(8,128)(2,1)} broadcast(bf16[192,512]{1,0:T(8,128)(2,1)S(1)} %bitcast.9), dimensions={1,2} | broadcast | bytes 1769472 | tf_op jit(solution)/shard_map/broadcast_in_dim | solution.py:414
  63.4 5.2 %all-to-all-start.3 = ((bf16[8,192,512]{2,1,0:T(8,128)(2,1)}), bf16[8,192,512]{2,1,0:T(8,128)(2,1)S(1)}, u32[]{:S(2)}, u32[]{:S(2)}) async-start(bf16[8,192,512]{2,1,0:T(8,128)(2,1)} %broadcast_in_dim.3), calls=%async_computation.3 | async-start | bytes 3145728 | tf_op jit(solution)/shard_map/all_to_all | solution.py:388
  68.6 0.0 collective-permute-start.1
  68.6 2.7 %collective-permute-done.1.got_ref = bf16[4,256,512]{2,1,0:T(8,128)(2,1)S(1)} collective-permute-done((bf16[4,256,512]{2,1,0:T(8,128)(2,1)S(1)}, bf16[4,256,512]{2,1,0:T(8,128)(2,1)S(1)}, u32[]{:S(2)}, u32[]{:S(2)}) %collective-permute-start.1) | collective-permute-done | bytes 1048608 | tf_op jit(solution)/shard_map/ppermute | solution.py:402
  71.3 0.0 copy-start
  71.3 1.0 copy-done
  72.2 1.0 tail.1
  73.2 4.9 %collective-permute-start.2 = (bf16[2,128,512]{2,1,0:T(8,128)(2,1)S(1)}, bf16[2,128,512]{2,1,0:T(8,128)(2,1)S(1)}, u32[]{:S(2)}, u32[]{:S(2)}) collective-permute-start(bf16[2,128,512]{2,1,0:T(8,128)(2,1)S(1)} %tail.1), channel_id=1, source_target_pairs={{0,4},{4,8},{8,12},{12,16},{16,20},{20,24},{24,28},{28,32},{32,36}... | collective-permute-start | bytes 786440 | tf_op jit(solution)/shard_map/ppermute | solution.py:411
  78.1 15.4 %collective-permute-done.2.halo_ref = bf16[2,128,512]{2,1,0:T(8,128)(2,1)S(1)} collective-permute-done((bf16[2,128,512]{2,1,0:T(8,128)(2,1)S(1)}, bf16[2,128,512]{2,1,0:T(8,128)(2,1)S(1)}, u32[]{:S(2)}, u32[]{:S(2)}) %collective-permute-start.2) | collective-permute-done | bytes 262176 | tf_op jit(solution)/shard_map/ppermute | solution.py:411
  93.5 4.3 %window_attention.1.att_ref = f32[512,512]{1,0:T(8,128)} custom-call(s32[1]{0:T(128)} %bitcast.place_ref, bf16[256,1024]{1,0:T(8,128)(2,1)} %own_q.1, bf16[256,1024]{1,0:T(8,128)(2,1)} %own_k.1, bf16[256,1024]{1,0:T(8,128)(2,1)} %own_v.1, bf16[4,256,512]{2,1,0:T(8,128)(2,1)} %copy-done, bf16[2,128,512]{2,1,0:T(8,128)(2,1)S(1)} %collective-permute-done.2.halo_ref), custom_call_target="tpu_custom_call" | custom-call | flops 268435456 | bytes 1572864 | tf_op jit(solution)/shard_map/window_attention/pallas_call | solution.py:275
  97.8 0.0 all-to-all-done.3
  97.8 7.4 %finish.1 = (bf16[128,512]{1,0:T(8,128)(2,1)S(1)}, bf16[128,512]{1,0:T(8,128)(2,1)S(1)}, bf16[128,512]{1,0:T(8,128)(2,1)S(1)}, bf16[128,512]{1,0:T(8,128)(2,1)S(1)}) custom-call(s32[1]{0:T(128)} %bitcast.place_ref, bf16[3,512,512]{2,1,0:T(8,128)(2,1)S(1)} %bitcast.6, bf16[2,512,512]{2,1,0:T(8,128)(2,1)} %gate_ref.1, bf16[2,512,512]{2,1,0:T(8,128)(2,1)} %up_ref.1, ...), custom_call_target="tpu_custom_call" | custom-call | flops 5637144576 | bytes 5242880 | tf_op jit(solution)/shard_map/finish/pallas_call | solution.py:344
  105.3 0.1 collective-permute-start.3
  105.4 0.8 collective-permute-start.4
  106.1 1.1 collective-permute-start.5
  107.2 0.0 collective-permute-done.3.refs_1_
  107.2 4.6 %collective-permute-done.4.refs_2_ = bf16[128,512]{1,0:T(8,128)(2,1)S(1)} collective-permute-done((bf16[128,512]{1,0:T(8,128)(2,1)S(1)}, bf16[128,512]{1,0:T(8,128)(2,1)S(1)}, u32[]{:S(2)}, u32[]{:S(2)}) %collective-permute-start.4) | collective-permute-done | bytes 131104 | tf_op jit(solution)/shard_map/ppermute | solution.py:418
  111.8 1.7 %collective-permute-done.5.refs_3_ = bf16[128,512]{1,0:T(8,128)(2,1)S(1)} collective-permute-done((bf16[128,512]{1,0:T(8,128)(2,1)S(1)}, bf16[128,512]{1,0:T(8,128)(2,1)S(1)}, u32[]{:S(2)}, u32[]{:S(2)}) %collective-permute-start.5) | collective-permute-done | bytes 131104 | tf_op jit(solution)/shard_map/ppermute | solution.py:419
  113.5 0.9 unpack.1
  (1 shorter events, 0.0 us)
Async XLA Ops:
  1.3 2.0 %collective-permute-start = (bf16[2,256,512]{2,1,0:T(8,128)(2,1)S(1)}, bf16[2,256,512]{2,1,0:T(8,128)(2,1)S(1)}, u32[]{:S(2)}, u32[]{:S(2)}) collective-permute-start(bf16[2,256,512]{2,1,0:T(8,128)(2,1)S(1)} %get-tuple-element.19), channel_id=1, source_target_pairs={{0,2},{2,0},{1,3},{3,1},{4,6},{6,4},{5,7},{7,5},{8,10},{10,8},{9,1... | collective-permute-start | bytes 1572872 | tf_op jit(solution)/shard_map/ppermute | solution.py:400
  63.4 34.4 %all-to-all-start.3 = ((bf16[8,192,512]{2,1,0:T(8,128)(2,1)}), bf16[8,192,512]{2,1,0:T(8,128)(2,1)S(1)}, u32[]{:S(2)}, u32[]{:S(2)}) async-start(bf16[8,192,512]{2,1,0:T(8,128)(2,1)} %broadcast_in_dim.3), calls=%async_computation.3 | async-start | bytes 3145728 | tf_op jit(solution)/shard_map/all_to_all | solution.py:388
  68.6 2.7 %collective-permute-start.1 = (bf16[4,256,512]{2,1,0:T(8,128)(2,1)S(1)}, bf16[4,256,512]{2,1,0:T(8,128)(2,1)S(1)}, u32[]{:S(2)}, u32[]{:S(2)}) collective-permute-start(bf16[4,256,512]{2,1,0:T(8,128)(2,1)S(1)} %get-tuple-element.24), channel_id=1, source_target_pairs={{0,2},{2,0},{1,3},{3,1},{4,6},{6,4},{5,7},{7,5},{8,10},{10,8},{9,1... | collective-permute-start | bytes 3145736 | tf_op jit(solution)/shard_map/ppermute | solution.py:402
  71.3 1.0 copy-start
  73.2 20.3 %collective-permute-start.2 = (bf16[2,128,512]{2,1,0:T(8,128)(2,1)S(1)}, bf16[2,128,512]{2,1,0:T(8,128)(2,1)S(1)}, u32[]{:S(2)}, u32[]{:S(2)}) collective-permute-start(bf16[2,128,512]{2,1,0:T(8,128)(2,1)S(1)} %tail.1), channel_id=1, source_target_pairs={{0,4},{4,8},{8,12},{12,16},{16,20},{20,24},{24,28},{28,32},{32,36}... | collective-permute-start | bytes 786440 | tf_op jit(solution)/shard_map/ppermute | solution.py:411
  105.3 2.0 %collective-permute-start.3 = (bf16[128,512]{1,0:T(8,128)(2,1)S(1)}, bf16[128,512]{1,0:T(8,128)(2,1)S(1)}, u32[]{:S(2)}, u32[]{:S(2)}) collective-permute-start(bf16[128,512]{1,0:T(8,128)(2,1)S(1)} %get-tuple-element.26), channel_id=1, source_target_pairs={{0,2},{2,0},{1,3},{3,1},{4,6},{6,4},{5,7},{7,5},{8,10},{10,8},{9,1... | collective-permute-start | bytes 393224 | tf_op jit(solution)/shard_map/ppermute | solution.py:420
  105.4 6.5 %collective-permute-start.4 = (bf16[128,512]{1,0:T(8,128)(2,1)S(1)}, bf16[128,512]{1,0:T(8,128)(2,1)S(1)}, u32[]{:S(2)}, u32[]{:S(2)}) collective-permute-start(bf16[128,512]{1,0:T(8,128)(2,1)S(1)} %get-tuple-element.27), channel_id=1, source_target_pairs={{0,1},{1,0},{2,3},{3,2},{4,5},{5,4},{6,7},{7,6},{8,9},{9,8},{10,11... | collective-permute-start | bytes 393224 | tf_op jit(solution)/shard_map/ppermute | solution.py:418
  106.1 7.4 %collective-permute-start.5 = (bf16[128,512]{1,0:T(8,128)(2,1)S(1)}, bf16[128,512]{1,0:T(8,128)(2,1)S(1)}, u32[]{:S(2)}, u32[]{:S(2)}) collective-permute-start(bf16[128,512]{1,0:T(8,128)(2,1)S(1)} %get-tuple-element.28), channel_id=1, source_target_pairs={{0,3},{1,2},{2,1},{3,0},{4,7},{5,6},{6,5},{7,4},{8,11},{9,10},{10,... | collective-permute-start | bytes 393224 | tf_op jit(solution)/shard_map/ppermute | solution.py:419

commit v2 on v1

--- a/solution.py
+++ b/solution.py
@@ -12,6 +12,7 @@
 NS_ITERS = 2
 DH = 512
 HALF = 256
+PARTS = 8
 
 linear_coef = 3.4445
 square_coef = -4.775
@@ -20,7 +21,7 @@
 
 
 CHIPS = ("z", "plane")
-ORDERS = {"plane": [0, 5, 2, 7, 4, 1, 6, 3], "z": [0, 2, 4, 6, 1, 3, 5, 7]}
+ORDERS = {"plane": [0, 5, 2, 7, 4, 1, 6, 3], "z": [7, 6, 5, 4, 3, 2, 1, 0]}
 QUAD = ("core", "yl")
 
 BF = jnp.bfloat16
@@ -153,9 +154,10 @@
         slope = sigmoid_gate * (1.0 + pre_gate * (1.0 - sigmoid_gate))
         gate_grad = (hidden_grad * pre_up * slope).astype(BF)
         up_grad = (hidden_grad * activated).astype(BF)
-        out_ref[0, :, cols] = mat(keys, gate_grad, TN).astype(BF)
-        out_ref[1, :, cols] = mat(keys, up_grad, TN).astype(BF)
-        out_ref[2, cols, :] = mat(hidden, out_grad, TN).astype(BF)
+        out_ref[:, 0, :, cols] = mat(keys, gate_grad, TN).astype(BF).reshape(PARTS, -1, HALF)
+        out_ref[:, 1, :, cols] = mat(keys, up_grad, TN).astype(BF).reshape(PARTS, -1, HALF)
+        down = mat(hidden, out_grad, TN).astype(BF).reshape(PARTS // 2, -1, DH)
+        out_ref[h * PARTS // 2 : (h + 1) * PARTS // 2, 2] = down
 
 
 def grads(own, got, weights):
@@ -164,7 +166,7 @@
         grads_body,
         in_specs=[VM] * 3,
         out_specs=VM,
-        out_shape=on_chip((3, DH, DH)),
+        out_shape=on_chip((PARTS, 3, DH // PARTS, DH)),
         compiler_params=PARAMS,
         cost_estimate=cost(12 * tokens * DH * DH, 8 * DH * DH * 2, tokens * DH),
         name="grads",
@@ -299,19 +301,20 @@
     return (stepped * (old_norm / new_norm)).astype(BF)
 
 
-def finish_body(
-    place_ref, sum_ref, gate_ref, up_ref, down_ref, own_ref, got_ref, att_ref, *rest
-):
-    out_refs = rest[:4]
-    all_ref, weight_ref, query_ref, attended_ref, sems = rest[4:]
-    core, yl, _ = seat(place_ref)
-    rows = own_ref.shape[0]
-    pairs = [(w.at[core], weight_ref.at[i]) for i, w in enumerate((gate_ref, up_ref, down_ref))]
-    pairs += [(half(own_ref, core), query_ref.at[0]), (got_ref.at[0], query_ref.at[1])]
-    copies = start_all(pairs + [(att_ref, attended_ref)], sems)
+MOVES = [(across, flip) for across in range(4) for flip in range(2)]
+
+
+def move_along(across, flip):
+    def target(p):
+        return ((p // 2 + across) % 4) * 2 + (p % 2 ^ flip)
+
+    return [(p, target(p)) for p in range(PARTS)]
+
+
+def orthogonal(gradients):
     iterates = []
-    for m in range(3):
-        gradient = sum_ref[m].astype(F32)
+    for gradient in gradients:
+        gradient = gradient.reshape(DH, DH).astype(F32)
         norm_total = jnp.sum(gradient * gradient)
         iterates.append((gradient * (1.0 / jnp.sqrt(norm_total + epsilon))).astype(BF))
     for _ in range(NS_ITERS):
@@ -323,15 +326,58 @@
             (linear_coef * x.astype(F32) + mat(p, x, NN)).astype(BF)
             for p, x in zip(polys, iterates)
         ]
+    return iterates
+
+
+def open_body(place_ref, sum_ref, gate_ref, up_ref, own_ref, got_ref, out_ref, *scratch):
+    weight_ref, query_ref, sems = scratch
+    core, _, _ = seat(place_ref)
+    rows = own_ref.shape[0]
+    pairs = [(w.at[core], weight_ref.at[i]) for i, w in enumerate((gate_ref, up_ref))]
+    for source, which in ((half(own_ref, core), core), (got_ref.at[0], 1 - core)):
+        place = pl.ds(pl.multiple_of(which * rows, rows), rows)
+        pairs.append((source, query_ref.at[place]))
+    copies = start_all(pairs, sems)
+    iterates = orthogonal([sum_ref[:, 0], sum_ref[:, 1]])
     wait_all(copies)
-    renewed = [refresh(weight_ref[i], x) for i, x in enumerate(iterates)]
-    for i, start in enumerate((core * rows, (1 - core) * rows)):
-        place = pl.ds(pl.multiple_of(start, rows), rows)
-        query_gate = mat(query_ref[i], renewed[0], NN)
-        query_up = mat(query_ref[i], renewed[1], NN)
-        query_hidden = (query_gate * jax.nn.sigmoid(query_gate) * query_up).astype(BF)
-        memory = mat(query_hidden, renewed[2], NN).astype(BF)
-        all_ref[place] = (memory.astype(F32) + attended_ref[place]).astype(BF)
+    gate, up = (refresh(weight_ref[i], x) for i, x in enumerate(iterates))
+    query_gate = mat(query_ref[...], gate, NN)
+    query_up = mat(query_ref[...], up, NN)
+    out_ref[...] = (query_gate * jax.nn.sigmoid(query_gate) * query_up).astype(BF)
+
+
+def open_answer(place, total, gate, up, own, got):
+    rows = own.shape[0]
+    return pl.pallas_call(
+        open_body,
+        in_specs=[SM, VM] + [HBM] * 4,
+        out_specs=VM,
+        out_shape=on_chip((2 * rows, DH)),
+        scratch_shapes=[
+            pltpu.VMEM((2, DH, DH), BF),
+            pltpu.VMEM((2 * rows, DH), BF),
+            pltpu.SemaphoreType.DMA((4,)),
+        ],
+        compiler_params=PARAMS,
+        cost_estimate=cost(28 * DH**3, 12 * DH * DH, rows * DH),
+        name="open_answer",
+    )(place, vmem(total), *hbm(gate, up, own, got))
+
+
+def close_body(place_ref, down_ref, hidden_ref, att_ref, *rest):
+    part_refs, out_refs = rest[:PARTS], rest[PARTS : PARTS + 4]
+    all_ref, sum_ref, weight_ref, attended_ref, sems = rest[PARTS + 4 :]
+    core, yl, chip = seat(place_ref)
+    copies = start_all([(down_ref.at[core], weight_ref), (att_ref, attended_ref)], sems)
+    x, yh = (chip >> 1) & 3, chip & 1
+    for ref, (across, flip) in zip(part_refs, MOVES):
+        source = ((x - across) & 3) * 2 + (yh ^ flip)
+        sum_ref[source ^ ((source & 1) * 4)] = ref[...]
+    (iterate,) = orthogonal([sum_ref[...]])
+    wait_all(copies)
+    down = refresh(weight_ref[...], iterate)
+    memory = mat(hidden_ref[...], down, NN).astype(BF)
+    all_ref[...] = (memory.astype(F32) + attended_ref[...]).astype(BF)
     block = out_refs[0].shape[0]
     for i, ref in enumerate(out_refs):
         to_core = 1 - core if i % 2 else core
@@ -339,24 +385,24 @@
         ref[...] = all_ref[pl.ds(pl.multiple_of((to_core * 2 + to_yl) * block, block), block)]
 
 
-def finish(place, total, gate, up, down, own, got, attended):
-    rows = own.shape[0]
-    return pl.pallas_call(
-        finish_body,
-        in_specs=[SM, VM] + [HBM] * 6,
+def close_answer(place, parts, down, hidden, attended):
+    rows = hidden.shape[0]
+    return pl.pallas_call(
+        close_body,
+        in_specs=[SM, HBM, VM, HBM] + [VM] * PARTS,
         out_specs=[VM] * 4,
-        out_shape=[on_chip((rows // 2, DH))] * 4,
+        out_shape=[on_chip((rows // 4, DH))] * 4,
         scratch_shapes=[
-            pltpu.VMEM((2 * rows, DH), BF),
-            pltpu.VMEM((3, DH, DH), BF),
-            pltpu.VMEM((2, rows, DH), BF),
-            pltpu.VMEM((2 * rows, DH), F32),
-            pltpu.SemaphoreType.DMA((6,)),
+            pltpu.VMEM((rows, DH), BF),
+            pltpu.VMEM((PARTS, DH // PARTS, DH), BF),
+            pltpu.VMEM((DH, DH), BF),
+            pltpu.VMEM((rows, DH), F32),
+            pltpu.SemaphoreType.DMA((2,)),
         ],
         compiler_params=PARAMS,
-        cost_estimate=cost(42 * DH**3, 20 * DH * DH, rows * DH),
-        name="finish",
-    )(place, vmem(total), *hbm(gate, up, down, own, got, attended))
+        cost_estimate=cost(14 * DH**3, 8 * DH * DH, 0),
+        name="close_answer",
+    )(place, *hbm(down), vmem(hidden), *hbm(attended), *[vmem(p) for p in parts])
 
 
 def unpack_body(place_ref, *refs):
@@ -411,10 +457,16 @@
     halo = lax.ppermute(last, CHIPS, [(s, s + 1) for s in range(chips - 1)])
     part = sum_spread(part)
     part = swap(part, "z").reshape(-1, DH)
-    spread = jnp.broadcast_to(part, (plane,) + part.shape)
-    total = swap(spread, "plane").reshape(3, DH, DH)
+    cut = 2 * DH // PARTS
+    first = jnp.broadcast_to(part[:cut], (plane, cut, DH))
+    first = swap(first, "plane").reshape(PARTS, 2, -1, DH)
+    second = part[cut:]
+    parts = [second] + [
+        lax.ppermute(second, "plane", move_along(*move)) for move in MOVES[1:]
+    ]
     attended = attend(place, rest[1:], got, halo)
-    kept, to_core, to_chip, to_both = finish(place, total, *weights, fw_q, got, attended)
+    hidden = open_answer(place, first, fast_gate, fast_up, fw_q, got)
+    kept, to_core, to_chip, to_both = close_answer(place, parts, fast_down, hidden, attended)
     from_chip = lax.ppermute(to_chip, "yl", pair)
     from_both = lax.ppermute(to_both, QUAD, [(s, 3 - s) for s in range(4)])
     from_core = lax.ppermute(to_core, "core", pair)

time: 116 us -> 121 us (1.043)
  the two profiles are of different devices: /device:TPU:4 before, /device:TPU:1 now
where the time goes in v2:
time: 121 us
  starting transfers between devices  42.6 us (35%)
  blocking collectives  37.5 us (31%)
  Pallas kernels  20.8 us (17%)
  waiting for transfers between devices  17.7 us (15%)
  local copies, waits for them, and re-layouts  2.07 us (2%)
    all_to_all x2, blocking collectives, swap(): lax.all_to_all(value, axis, split_axis=0, concat_axis=0, tiled=True, axis...  37.5 us
    ppermute x7, starting transfers between devices, step(): lax.ppermute(second, 'plane', move_along(*move))  15.3 us
    all_to_all x2, starting transfers between devices, swap(): lax.all_to_all(value, axis, split_axis=0, concat_axis=0, tiled=True, axis...  13 us
    ppermute x1, waiting for transfers between devices, step(): halo = lax.ppermute(last, CHIPS, [(s, s + 1) for s in range(chips - 1)])  8.01 us
    pallas_call x1, Pallas kernels, open_answer(): pl.pallas_call(open_body, in_specs=[SM, VM] + [HBM] * 4, out_specs=VM, ou...  5.07 us
    ppermute x1, starting transfers between devices, step(): halo = lax.ppermute(last, CHIPS, [(s, s + 1) for s in range(chips - 1)])  4.88 us
    pallas_call x1, Pallas kernels, attend(): pl.pallas_call(attend_body, in_specs=[SM, HBM, HBM, HBM, HBM, VM], out_sp...  4.29 us
    all_to_all x2, waiting for transfers between devices, swap(): lax.all_to_all(value, axis, split_axis=0, concat_axis=0, tiled=True, axis...  3.37 us
  transfers between devices with their start and end apart: 15, of which 4 were waited for; matrix products, arithmetic and copies ran while one was open for 1% of the time, Pallas kernels for 10%

profile of v2, /device:TPU:1, one launch (start us, length us, event | category | flops | bytes accessed | tf_op | source)
XLA Modules:
  0.0 120.8 jit_solution(14370203781986980358)
XLA Ops:
  0.0 1.3 %pack_grad.1 = (bf16[2,256,512]{2,1,0:T(8,128)(2,1)S(1)}, bf16[2,256,512]{2,1,0:T(8,128)(2,1)S(1)}) custom-call(s32[1]{0:T(128)} %bitcast.place_ref, bf16[256,1024]{1,0:T(8,128)(2,1)} %k_ref.2, bf16[256,1024]{1,0:T(8,128)(2,1)} %v_ref.2, f32[2,256]{1,0:T(2,128)} %bitcast.10), custom_call_target="tpu_custom_call" | custom-call | flops 262144 | bytes 2097152 | tf_op jit(solution)/shard_map/pack_grad/pallas_call | solution.py:105
  1.3 3.3 %collective-permute-start = (bf16[2,256,512]{2,1,0:T(8,128)(2,1)S(1)}, bf16[2,256,512]{2,1,0:T(8,128)(2,1)S(1)}, u32[]{:S(2)}, u32[]{:S(2)}) collective-permute-start(bf16[2,256,512]{2,1,0:T(8,128)(2,1)S(1)} %get-tuple-element.19), channel_id=1, source_target_pairs={{0,2},{2,0},{1,3},{3,1},{4,6},{6,4},{5,7},{7,5},{8,10},{10,8},{9,1... | collective-permute-start | bytes 1572872 | tf_op jit(solution)/shard_map/ppermute | solution.py:446
  4.6 1.7 %pick.1 = (bf16[3,512,512]{2,1,0:T(8,128)(2,1)S(1)}, bf16[4,256,512]{2,1,0:T(8,128)(2,1)S(1)}) custom-call(s32[1]{0:T(128)} %bitcast.place_ref, bf16[2,512,512]{2,1,0:T(8,128)(2,1)} %gate_ref.1, bf16[2,512,512]{2,1,0:T(8,128)(2,1)} %up_ref.1, bf16[2,512,512]{2,1,0:T(8,128)(2,1)} %down_ref.1, bf16[256,1024]{1,0:T(8,128)(2,1)} %own_ref.1, ...), custom_call_target="tpu_custom_call" | custom-call | bytes 2621440 | tf_op jit(solution)/shard_map/pick/pallas_call | solution.py:131
  6.3 0.0 collective-permute-done.got_ref
  6.3 2.3 %grads.1 = bf16[8,3,64,512]{3,2,1,0:T(8,128)(2,1)S(1)} custom-call(bf16[2,256,512]{2,1,0:T(8,128)(2,1)S(1)} %get-tuple-element.17.own_ref, bf16[2,256,512]{2,1,0:T(8,128)(2,1)S(1)} %collective-permute-done.got_ref, bf16[3,512,512]{2,1,0:T(8,128)(2,1)S(1)} %get-tuple-element.23.weight_ref), custom_call_target="tpu_custom_call" | custom-call | flops 1610612736 | bytes 4194304 | tf_op jit(solution)/shard_map/grads/pallas_call | solution.py:165
  8.6 26.5 %all_to_all.20.in_ref = bf16[8,192,512]{2,1,0:T(8,128)(2,1)S(1)} all-to-all(bf16[8,192,512]{2,1,0:T(8,128)(2,1)S(1)} %bitcast.6), channel_id=1, replica_groups={{0,20,8,28,16,4,24,12},{1,21,9,29,17,5,25,13},{2,22,10,30,18,6,26,14},{..., dimensions={0} | all-to-all | bytes 3145728 | tf_op jit(solution)/shard_map/all_to_all | solution.py:434
  35.1 0.9 plane_sum.1
  36.0 9.0 %all-to-all-start.1 = ((bf16[8,24,512]{2,1,0:T(8,128)(2,1)}), bf16[8,24,512]{2,1,0:T(8,128)(2,1)S(1)}, u32[]{:S(2)}, u32[]{:S(2)}) async-start(bf16[8,24,512]{2,1,0:T(8,128)(2,1)} %bitcast.3), calls=%async_computation.1 | async-start | bytes 393216 | tf_op jit(solution)/shard_map/all_to_all | solution.py:434
  45.0 1.9 %collective-permute-start.1 = (bf16[4,256,512]{2,1,0:T(8,128)(2,1)S(1)}, bf16[4,256,512]{2,1,0:T(8,128)(2,1)S(1)}, u32[]{:S(2)}, u32[]{:S(2)}) collective-permute-start(bf16[4,256,512]{2,1,0:T(8,128)(2,1)S(1)} %get-tuple-element.24), channel_id=1, source_target_pairs={{0,2},{2,0},{1,3},{3,1},{4,6},{6,4},{5,7},{7,5},{8,10},{10,8},{9,1... | collective-permute-start | bytes 3145736 | tf_op jit(solution)/shard_map/ppermute | solution.py:448
  46.9 3.4 %all-to-all-done.1.in_ref = bf16[8,24,512]{2,1,0:T(8,128)(2,1)S(1)} async-done(((bf16[8,24,512]{2,1,0:T(8,128)(2,1)}), bf16[8,24,512]{2,1,0:T(8,128)(2,1)S(1)}, u32[]{:S(2)}, u32[]{:S(2)}) %all-to-all-start.1) | async-done | bytes 196640 | tf_op jit(solution)/shard_map/all_to_all | solution.py:434
  50.3 11.0 %all_to_all.21 = bf16[8,24,512]{2,1,0:T(8,128)(2,1)S(1)} all-to-all(bf16[8,24,512]{2,1,0:T(8,128)(2,1)S(1)} %depth_sum.1), channel_id=1, replica_groups={{224,192,160,128,96,64,32,0},{225,193,161,129,97,65,33,1},{226,194,162,..., dimensions={0} | all-to-all | bytes 393216 | tf_op jit(solution)/shard_map/all_to_all | solution.py:434
  61.2 1.1 broadcast_in_dim.3
  62.3 4.1 %all-to-all-start.3 = ((bf16[8,128,512]{2,1,0:T(8,128)(2,1)}), bf16[8,128,512]{2,1,0:T(8,128)(2,1)S(1)}, u32[]{:S(2)}, u32[]{:S(2)}) async-start(bf16[8,128,512]{2,1,0:T(8,128)(2,1)} %broadcast_in_dim.3), calls=%async_computation.3 | async-start | bytes 2097152 | tf_op jit(solution)/shard_map/all_to_all | solution.py:434
  66.4 0.0 collective-permute-done.1.got_ref
  66.4 0.0 copy-start
  66.4 1.0 copy-done
  67.4 1.0 tail.1
  68.4 4.9 %collective-permute-start.2 = (bf16[2,128,512]{2,1,0:T(8,128)(2,1)S(1)}, bf16[2,128,512]{2,1,0:T(8,128)(2,1)S(1)}, u32[]{:S(2)}, u32[]{:S(2)}) collective-permute-start(bf16[2,128,512]{2,1,0:T(8,128)(2,1)S(1)} %tail.1), channel_id=1, source_target_pairs={{0,4},{4,8},{8,12},{12,16},{16,20},{20,24},{24,28},{28,32},{32,36}... | collective-permute-start | bytes 786440 | tf_op jit(solution)/shard_map/ppermute | solution.py:457
  73.3 3.0 %collective-permute-start.9 = (bf16[64,512]{1,0:T(8,128)(2,1)S(1)}, bf16[64,512]{1,0:T(8,128)(2,1)S(1)}, u32[]{:S(2)}, u32[]{:S(2)}) collective-permute-start(bf16[64,512]{1,0:T(8,128)(2,1)S(1)} %slice.9.rest_0_), channel_id=1, source_target_pairs={{0,28},{4,24},{8,4},{12,0},{16,12},{20,8},{24,20},{28,16},{1,29},{... | collective-permute-start | bytes 196616 | tf_op jit(solution)/shard_map/ppermute | solution.py:465
  76.3 0.6 collective-permute-start.8
  76.9 8.0 %collective-permute-done.2.halo_ref = bf16[2,128,512]{2,1,0:T(8,128)(2,1)S(1)} collective-permute-done((bf16[2,128,512]{2,1,0:T(8,128)(2,1)S(1)}, bf16[2,128,512]{2,1,0:T(8,128)(2,1)S(1)}, u32[]{:S(2)}, u32[]{:S(2)}) %collective-permute-start.2) | collective-permute-done | bytes 262176 | tf_op jit(solution)/shard_map/ppermute | solution.py:457
  85.0 4.3 %window_attention.1.att_ref = f32[512,512]{1,0:T(8,128)} custom-call(s32[1]{0:T(128)} %bitcast.place_ref, bf16[256,1024]{1,0:T(8,128)(2,1)} %own_q.1, bf16[256,1024]{1,0:T(8,128)(2,1)} %own_k.1, bf16[256,1024]{1,0:T(8,128)(2,1)} %own_v.1, bf16[4,256,512]{2,1,0:T(8,128)(2,1)} %copy-done, bf16[2,128,512]{2,1,0:T(8,128)(2,1)S(1)} %collective-permute-done.2.halo_ref), custom_call_target="tpu_custom_call" | custom-call | flops 268435456 | bytes 1572864 | tf_op jit(solution)/shard_map/window_attention/pallas_call | solution.py:277
  89.3 6.3 %collective-permute-start.7 = (bf16[64,512]{1,0:T(8,128)(2,1)S(1)}, bf16[64,512]{1,0:T(8,128)(2,1)S(1)}, u32[]{:S(2)}, u32[]{:S(2)}) collective-permute-start(bf16[64,512]{1,0:T(8,128)(2,1)S(1)} %slice.9.rest_0_), channel_id=1, source_target_pairs={{0,20},{4,16},{8,28},{12,24},{16,4},{20,0},{24,12},{28,8},{1,21},{... | collective-permute-start | bytes 196616 | tf_op jit(solution)/shard_map/ppermute | solution.py:465
  95.6 0.2 collective-permute-start.6
  95.7 0.0 collective-permute-start.5
  95.7 0.0 collective-permute-done.9.rest_7_
  95.7 1.5 %collective-permute-start.4 = (bf16[64,512]{1,0:T(8,128)(2,1)S(1)}, bf16[64,512]{1,0:T(8,128)(2,1)S(1)}, u32[]{:S(2)}, u32[]{:S(2)}) collective-permute-start(bf16[64,512]{1,0:T(8,128)(2,1)S(1)} %slice.9.rest_0_), channel_id=1, source_target_pairs={{0,8},{4,12},{8,16},{12,20},{16,24},{20,28},{24,0},{28,4},{1,9},{5... | collective-permute-start | bytes 196616 | tf_op jit(solution)/shard_map/ppermute | solution.py:465
  97.2 0.0 collective-permute-done.8.rest_6_
  97.2 3.7 %collective-permute-start.3 = (bf16[64,512]{1,0:T(8,128)(2,1)S(1)}, bf16[64,512]{1,0:T(8,128)(2,1)S(1)}, u32[]{:S(2)}, u32[]{:S(2)}) collective-permute-start(bf16[64,512]{1,0:T(8,128)(2,1)S(1)} %slice.9.rest_0_), channel_id=1, source_target_pairs={{0,4},{4,0},{8,12},{12,8},{16,20},{20,16},{24,28},{28,24},{1,5},{5... | collective-permute-start | bytes 196616 | tf_op jit(solution)/shard_map/ppermute | solution.py:465
  100.9 0.0 all-to-all-done.3
  100.9 5.1 %open_answer.1.hidden_ref = bf16[512,512]{1,0:T(8,128)(2,1)S(1)} custom-call(s32[1]{0:T(128)} %bitcast.place_ref, bf16[8,2,64,512]{3,2,1,0:T(8,128)(2,1)S(1)} %bitcast.7, bf16[2,512,512]{2,1,0:T(8,128)(2,1)} %gate_ref.1, bf16[2,512,512]{2,1,0:T(8,128)(2,1)} %up_ref.1, bf16[256,1024]{1,0:T(8,128)(2,1)} %own_ref.1, bf16[4,256,512]{2,1,0:T(8,128)(2,1)} %copy-done), custom_call_target="tpu_custom_call" | custom-call | flops 3758096384 | bytes 3145728 | tf_op jit(solution)/shard_map/open_answer/pallas_call | solution.py:351
  106.0 0.0 collective-permute-done.7.rest_5_
  106.0 0.0 collective-permute-done.6.rest_4_
  106.0 0.0 collective-permute-done.5.rest_3_
  106.0 0.0 collective-permute-done.4.rest_2_
  106.0 0.0 collective-permute-done.3.rest_1_
  106.0 3.3 %close_answer.1 = (bf16[128,512]{1,0:T(8,128)(2,1)S(1)}, bf16[128,512]{1,0:T(8,128)(2,1)S(1)}, bf16[128,512]{1,0:T(8,128)(2,1)S(1)}, bf16[128,512]{1,0:T(8,128)(2,1)S(1)}) custom-call(s32[1]{0:T(128)} %bitcast.place_ref, bf16[2,512,512]{2,1,0:T(8,128)(2,1)} %down_ref.1, bf16[512,512]{1,0:T(8,128)(2,1)S(1)} %open_answer.1.hidden_ref, ...), custom_call_target="tpu_custom_call" | custom-call | flops 1879048192 | bytes 2097152 | tf_op jit(solution)/shard_map/close_answer/pallas_call | solution.py:390
  109.4 2.5 %collective-permute-start.10 = (bf16[128,512]{1,0:T(8,128)(2,1)S(1)}, bf16[128,512]{1,0:T(8,128)(2,1)S(1)}, u32[]{:S(2)}, u32[]{:S(2)}) collective-permute-start(bf16[128,512]{1,0:T(8,128)(2,1)S(1)} %get-tuple-element.26), channel_id=1, source_target_pairs={{0,2},{2,0},{1,3},{3,1},{4,6},{6,4},{5,7},{7,5},{8,10},{10,8},{9,1... | collective-permute-start | bytes 393224 | tf_op jit(solution)/shard_map/ppermute | solution.py:472
  111.9 0.4 collective-permute-start.11
  112.3 1.3 %collective-permute-start.12 = (bf16[128,512]{1,0:T(8,128)(2,1)S(1)}, bf16[128,512]{1,0:T(8,128)(2,1)S(1)}, u32[]{:S(2)}, u32[]{:S(2)}) collective-permute-start(bf16[128,512]{1,0:T(8,128)(2,1)S(1)} %get-tuple-element.28), channel_id=1, source_target_pairs={{0,3},{1,2},{2,1},{3,0},{4,7},{5,6},{6,5},{7,4},{8,11},{9,10},{10,... | collective-permute-start | bytes 393224 | tf_op jit(solution)/shard_map/ppermute | solution.py:471
  113.6 0.0 collective-permute-done.10.refs_1_
  113.6 3.2 %collective-permute-done.11.refs_2_ = bf16[128,512]{1,0:T(8,128)(2,1)S(1)} collective-permute-done((bf16[128,512]{1,0:T(8,128)(2,1)S(1)}, bf16[128,512]{1,0:T(8,128)(2,1)S(1)}, u32[]{:S(2)}, u32[]{:S(2)}) %collective-permute-start.11) | collective-permute-done | bytes 131104 | tf_op jit(solution)/shard_map/ppermute | solution.py:470
  116.8 3.1 %collective-permute-done.12.refs_3_ = bf16[128,512]{1,0:T(8,128)(2,1)S(1)} collective-permute-done((bf16[128,512]{1,0:T(8,128)(2,1)S(1)}, bf16[128,512]{1,0:T(8,128)(2,1)S(1)}, u32[]{:S(2)}, u32[]{:S(2)}) %collective-permute-start.12) | collective-permute-done | bytes 131104 | tf_op jit(solution)/shard_map/ppermute | solution.py:471
  119.9 0.9 unpack.1
  (3 shorter events, 0.0 us)
Async XLA Ops:
  1.3 5.0 %collective-permute-start = (bf16[2,256,512]{2,1,0:T(8,128)(2,1)S(1)}, bf16[2,256,512]{2,1,0:T(8,128)(2,1)S(1)}, u32[]{:S(2)}, u32[]{:S(2)}) collective-permute-start(bf16[2,256,512]{2,1,0:T(8,128)(2,1)S(1)} %get-tuple-element.19), channel_id=1, source_target_pairs={{0,2},{2,0},{1,3},{3,1},{4,6},{6,4},{5,7},{7,5},{8,10},{10,8},{9,1... | collective-permute-start | bytes 1572872 | tf_op jit(solution)/shard_map/ppermute | solution.py:446
  36.0 14.2 %all-to-all-start.1 = ((bf16[8,24,512]{2,1,0:T(8,128)(2,1)}), bf16[8,24,512]{2,1,0:T(8,128)(2,1)S(1)}, u32[]{:S(2)}, u32[]{:S(2)}) async-start(bf16[8,24,512]{2,1,0:T(8,128)(2,1)} %bitcast.3), calls=%async_computation.1 | async-start | bytes 393216 | tf_op jit(solution)/shard_map/all_to_all | solution.py:434
  45.0 21.5 %collective-permute-start.1 = (bf16[4,256,512]{2,1,0:T(8,128)(2,1)S(1)}, bf16[4,256,512]{2,1,0:T(8,128)(2,1)S(1)}, u32[]{:S(2)}, u32[]{:S(2)}) collective-permute-start(bf16[4,256,512]{2,1,0:T(8,128)(2,1)S(1)} %get-tuple-element.24), channel_id=1, source_target_pairs={{0,2},{2,0},{1,3},{3,1},{4,6},{6,4},{5,7},{7,5},{8,10},{10,8},{9,1... | collective-permute-start | bytes 3145736 | tf_op jit(solution)/shard_map/ppermute | solution.py:448
  62.3 38.6 %all-to-all-start.3 = ((bf16[8,128,512]{2,1,0:T(8,128)(2,1)}), bf16[8,128,512]{2,1,0:T(8,128)(2,1)S(1)}, u32[]{:S(2)}, u32[]{:S(2)}) async-start(bf16[8,128,512]{2,1,0:T(8,128)(2,1)} %broadcast_in_dim.3), calls=%async_computation.3 | async-start | bytes 2097152 | tf_op jit(solution)/shard_map/all_to_all | solution.py:434
  66.4 1.0 copy-start
  68.4 16.6 %collective-permute-start.2 = (bf16[2,128,512]{2,1,0:T(8,128)(2,1)S(1)}, bf16[2,128,512]{2,1,0:T(8,128)(2,1)S(1)}, u32[]{:S(2)}, u32[]{:S(2)}) collective-permute-start(bf16[2,128,512]{2,1,0:T(8,128)(2,1)S(1)} %tail.1), channel_id=1, source_target_pairs={{0,4},{4,8},{8,12},{12,16},{16,20},{20,24},{24,28},{28,32},{32,36}... | collective-permute-start | bytes 786440 | tf_op jit(solution)/shard_map/ppermute | solution.py:457
  73.3 22.4 %collective-permute-start.9 = (bf16[64,512]{1,0:T(8,128)(2,1)S(1)}, bf16[64,512]{1,0:T(8,128)(2,1)S(1)}, u32[]{:S(2)}, u32[]{:S(2)}) collective-permute-start(bf16[64,512]{1,0:T(8,128)(2,1)S(1)} %slice.9.rest_0_), channel_id=1, source_target_pairs={{0,28},{4,24},{8,4},{12,0},{16,12},{20,8},{24,20},{28,16},{1,29},{... | collective-permute-start | bytes 196616 | tf_op jit(solution)/shard_map/ppermute | solution.py:465
  76.3 20.8 %collective-permute-start.8 = (bf16[64,512]{1,0:T(8,128)(2,1)S(1)}, bf16[64,512]{1,0:T(8,128)(2,1)S(1)}, u32[]{:S(2)}, u32[]{:S(2)}) collective-permute-start(bf16[64,512]{1,0:T(8,128)(2,1)S(1)} %slice.9.rest_0_), channel_id=1, source_target_pairs={{0,24},{4,28},{8,0},{12,4},{16,8},{20,12},{24,16},{28,20},{1,25},{... | collective-permute-start | bytes 196616 | tf_op jit(solution)/shard_map/ppermute | solution.py:465
  89.3 16.7 %collective-permute-start.7 = (bf16[64,512]{1,0:T(8,128)(2,1)S(1)}, bf16[64,512]{1,0:T(8,128)(2,1)S(1)}, u32[]{:S(2)}, u32[]{:S(2)}) collective-permute-start(bf16[64,512]{1,0:T(8,128)(2,1)S(1)} %slice.9.rest_0_), channel_id=1, source_target_pairs={{0,20},{4,16},{8,28},{12,24},{16,4},{20,0},{24,12},{28,8},{1,21},{... | collective-permute-start | bytes 196616 | tf_op jit(solution)/shard_map/ppermute | solution.py:465
  95.6 10.4 %collective-permute-start.6 = (bf16[64,512]{1,0:T(8,128)(2,1)S(1)}, bf16[64,512]{1,0:T(8,128)(2,1)S(1)}, u32[]{:S(2)}, u32[]{:S(2)}) collective-permute-start(bf16[64,512]{1,0:T(8,128)(2,1)S(1)} %slice.9.rest_0_), channel_id=1, source_target_pairs={{0,16},{4,20},{8,24},{12,28},{16,0},{20,4},{24,8},{28,12},{1,17},{... | collective-permute-start | bytes 196616 | tf_op jit(solution)/shard_map/ppermute | solution.py:465
  95.7 10.3 %collective-permute-start.5 = (bf16[64,512]{1,0:T(8,128)(2,1)S(1)}, bf16[64,512]{1,0:T(8,128)(2,1)S(1)}, u32[]{:S(2)}, u32[]{:S(2)}) collective-permute-start(bf16[64,512]{1,0:T(8,128)(2,1)S(1)} %slice.9.rest_0_), channel_id=1, source_target_pairs={{0,12},{4,8},{8,20},{12,16},{16,28},{20,24},{24,4},{28,0},{1,13},{... | collective-permute-start | bytes 196616 | tf_op jit(solution)/shard_map/ppermute | solution.py:465
  95.7 10.3 %collective-permute-start.4 = (bf16[64,512]{1,0:T(8,128)(2,1)S(1)}, bf16[64,512]{1,0:T(8,128)(2,1)S(1)}, u32[]{:S(2)}, u32[]{:S(2)}) collective-permute-start(bf16[64,512]{1,0:T(8,128)(2,1)S(1)} %slice.9.rest_0_), channel_id=1, source_target_pairs={{0,8},{4,12},{8,16},{12,20},{16,24},{20,28},{24,0},{28,4},{1,9},{5... | collective-permute-start | bytes 196616 | tf_op jit(solution)/shard_map/ppermute | solution.py:465
  97.2 8.8 %collective-permute-start.3 = (bf16[64,512]{1,0:T(8,128)(2,1)S(1)}, bf16[64,512]{1,0:T(8,128)(2,1)S(1)}, u32[]{:S(2)}, u32[]{:S(2)}) collective-permute-start(bf16[64,512]{1,0:T(8,128)(2,1)S(1)} %slice.9.rest_0_), channel_id=1, source_target_pairs={{0,4},{4,0},{8,12},{12,8},{16,20},{20,16},{24,28},{28,24},{1,5},{5... | collective-permute-start | bytes 196616 | tf_op jit(solution)/shard_map/ppermute | solution.py:465
  109.4 4.2 %collective-permute-start.10 = (bf16[128,512]{1,0:T(8,128)(2,1)S(1)}, bf16[128,512]{1,0:T(8,128)(2,1)S(1)}, u32[]{:S(2)}, u32[]{:S(2)}) collective-permute-start(bf16[128,512]{1,0:T(8,128)(2,1)S(1)} %get-tuple-element.26), channel_id=1, source_target_pairs={{0,2},{2,0},{1,3},{3,1},{4,6},{6,4},{5,7},{7,5},{8,10},{10,8},{9,1... | collective-permute-start | bytes 393224 | tf_op jit(solution)/shard_map/ppermute | solution.py:472
  111.9 5.0 %collective-permute-start.11 = (bf16[128,512]{1,0:T(8,128)(2,1)S(1)}, bf16[128,512]{1,0:T(8,128)(2,1)S(1)}, u32[]{:S(2)}, u32[]{:S(2)}) collective-permute-start(bf16[128,512]{1,0:T(8,128)(2,1)S(1)} %get-tuple-element.27), channel_id=1, source_target_pairs={{0,1},{1,0},{2,3},{3,2},{4,5},{5,4},{6,7},{7,6},{8,9},{9,8},{10,11... | collective-permute-start | bytes 393224 | tf_op jit(solution)/shard_map/ppermute | solution.py:470
  112.3 7.6 %collective-permute-start.12 = (bf16[128,512]{1,0:T(8,128)(2,1)S(1)}, bf16[128,512]{1,0:T(8,128)(2,1)S(1)}, u32[]{:S(2)}, u32[]{:S(2)}) collective-permute-start(bf16[128,512]{1,0:T(8,128)(2,1)S(1)} %get-tuple-element.28), channel_id=1, source_target_pairs={{0,3},{1,2},{2,1},{3,0},{4,7},{5,6},{6,5},{7,4},{8,11},{9,10},{10,... | collective-permute-start | bytes 393224 | tf_op jit(solution)/shard_map/ppermute | solution.py:471

commit v3 on v2

--- a/solution.py
+++ b/solution.py
@@ -236,6 +236,28 @@
         cost_estimate=cost(parts.size, 4 * parts.size),
         name="depth_sum",
     )(vmem(parts))
+
+
+def spread_body(in_ref, out_ref, rest_ref, sems):
+    cut = out_ref.shape[1]
+    copies = start_all([(in_ref.at[:cut], out_ref.at[i]) for i in range(PARTS)], sems)
+    rest_ref[...] = in_ref[cut:]
+    wait_all(copies)
+
+
+def spread(part):
+    rows = part.shape[0]
+    cut = 2 * rows // 3
+    return pl.pallas_call(
+        spread_body,
+        in_specs=[VM],
+        out_specs=[HBM, VM],
+        out_shape=[pltpu.HBM((PARTS, cut, DH), BF), on_chip((rows - cut, DH))],
+        scratch_shapes=[pltpu.SemaphoreType.DMA((PARTS,))],
+        compiler_params=PARAMS,
+        cost_estimate=cost(0, 2 * (PARTS + 1) * part.size),
+        name="spread",
+    )(vmem(part))
 
 
 def attend_body(place_ref, own_q, own_k, own_v, got_ref, halo_ref, out_ref, *scratch):
@@ -301,7 +323,7 @@
     return (stepped * (old_norm / new_norm)).astype(BF)
 
 
-MOVES = [(across, flip) for across in range(4) for flip in range(2)]
+MOVES = [(0, 0), (0, 1), (2, 1), (2, 0), (1, 1), (3, 1), (1, 0), (3, 0)]
 
 
 def move_along(across, flip):
@@ -457,10 +479,8 @@
     halo = lax.ppermute(last, CHIPS, [(s, s + 1) for s in range(chips - 1)])
     part = sum_spread(part)
     part = swap(part, "z").reshape(-1, DH)
-    cut = 2 * DH // PARTS
-    first = jnp.broadcast_to(part[:cut], (plane, cut, DH))
+    first, second = spread(part)
     first = swap(first, "plane").reshape(PARTS, 2, -1, DH)
-    second = part[cut:]
     parts = [second] + [
         lax.ppermute(second, "plane", move_along(*move)) for move in MOVES[1:]
     ]

time: 121 us -> 124 us (1.025)
  the two profiles are of different devices: /device:TPU:1 before, /device:TPU:4 now
where the time goes in v3:
time: 124 us; the launch traced here: 122 us
  blocking collectives  39.6 us (32%)
  starting transfers between devices  35.5 us (29%)
  waiting for transfers between devices  23.5 us (19%)
  Pallas kernels  21.8 us (18%)
    all_to_all x2, blocking collectives, swap(): lax.all_to_all(value, axis, split_axis=0, concat_axis=0, tiled=True, axis...  39.6 us
    all_to_all x2, starting transfers between devices, swap(): lax.all_to_all(value, axis, split_axis=0, concat_axis=0, tiled=True, axis...  15.5 us
    ppermute x7, starting transfers between devices, step(): lax.ppermute(second, 'plane', move_along(*move))  13.1 us
    ppermute x1, waiting for transfers between devices, step(): halo = lax.ppermute(last, CHIPS, [(s, s + 1) for s in range(chips - 1)])  9.99 us
    all_to_all x2, waiting for transfers between devices, swap(): lax.all_to_all(value, axis, split_axis=0, concat_axis=0, tiled=True, axis...  7.08 us
    pallas_call x1, Pallas kernels, open_answer(): pl.pallas_call(open_body, in_specs=[SM, VM] + [HBM] * 4, out_specs=VM, ou...  5.08 us
    ppermute x1, starting transfers between devices, step(): halo = lax.ppermute(last, CHIPS, [(s, s + 1) for s in range(chips - 1)])  4.87 us
    ppermute x1, waiting for transfers between devices, step(): from_chip = lax.ppermute(to_chip, 'yl', pair)  4.61 us
  transfers between devices with their start and end apart: 15, of which 5 were waited for; matrix products, arithmetic and copies ran while one was open for 0% of the time, Pallas kernels for 11%

profile of v3, /device:TPU:4, one launch (start us, length us, event | category | flops | bytes accessed | tf_op | source)
XLA Modules:
  0.0 121.6 jit_solution(13439192564773404954)
XLA Ops:
  0.0 1.3 %pack_grad.1 = (bf16[2,256,512]{2,1,0:T(8,128)(2,1)S(1)}, bf16[2,256,512]{2,1,0:T(8,128)(2,1)S(1)}) custom-call(s32[1]{0:T(128)} %bitcast.place_ref, bf16[256,1024]{1,0:T(8,128)(2,1)} %k_ref.2, bf16[256,1024]{1,0:T(8,128)(2,1)} %v_ref.2, f32[2,256]{1,0:T(2,128)} %bitcast.9), custom_call_target="tpu_custom_call" | custom-call | flops 262144 | bytes 2097152 | tf_op jit(solution)/shard_map/pack_grad/pallas_call | solution.py:105
  1.3 0.1 collective-permute-start
  1.4 1.7 %pick.1 = (bf16[3,512,512]{2,1,0:T(8,128)(2,1)S(1)}, bf16[4,256,512]{2,1,0:T(8,128)(2,1)S(1)}) custom-call(s32[1]{0:T(128)} %bitcast.place_ref, bf16[2,512,512]{2,1,0:T(8,128)(2,1)} %gate_ref.1, bf16[2,512,512]{2,1,0:T(8,128)(2,1)} %up_ref.1, bf16[2,512,512]{2,1,0:T(8,128)(2,1)} %down_ref.1, bf16[256,1024]{1,0:T(8,128)(2,1)} %own_ref.1, ...), custom_call_target="tpu_custom_call" | custom-call | bytes 2621440 | tf_op jit(solution)/shard_map/pick/pallas_call | solution.py:131
  3.1 0.1 collective-permute-done.got_ref
  3.3 2.3 %grads.1 = bf16[8,3,64,512]{3,2,1,0:T(8,128)(2,1)S(1)} custom-call(bf16[2,256,512]{2,1,0:T(8,128)(2,1)S(1)} %get-tuple-element.19.own_ref, bf16[2,256,512]{2,1,0:T(8,128)(2,1)S(1)} %collective-permute-done.got_ref, bf16[3,512,512]{2,1,0:T(8,128)(2,1)S(1)} %get-tuple-element.25.weight_ref), custom_call_target="tpu_custom_call" | custom-call | flops 1610612736 | bytes 4194304 | tf_op jit(solution)/shard_map/grads/pallas_call | solution.py:165
  5.6 28.2 %all_to_all.20.in_ref = bf16[8,192,512]{2,1,0:T(8,128)(2,1)S(1)} all-to-all(bf16[8,192,512]{2,1,0:T(8,128)(2,1)S(1)} %bitcast.6), channel_id=1, replica_groups={{0,20,8,28,16,4,24,12},{1,21,9,29,17,5,25,13},{2,22,10,30,18,6,26,14},{..., dimensions={0} | all-to-all | bytes 3145728 | tf_op jit(solution)/shard_map/all_to_all | solution.py:456
  33.7 0.9 plane_sum.1
  34.6 9.2 %all-to-all-start.1 = ((bf16[8,24,512]{2,1,0:T(8,128)(2,1)}), bf16[8,24,512]{2,1,0:T(8,128)(2,1)S(1)}, u32[]{:S(2)}, u32[]{:S(2)}) async-start(bf16[8,24,512]{2,1,0:T(8,128)(2,1)} %bitcast.3), calls=%async_computation.1 | async-start | bytes 393216 | tf_op jit(solution)/shard_map/all_to_all | solution.py:456
  43.8 0.0 collective-permute-start.1
  43.8 7.1 %all-to-all-done.1.in_ref = bf16[8,24,512]{2,1,0:T(8,128)(2,1)S(1)} async-done(((bf16[8,24,512]{2,1,0:T(8,128)(2,1)}), bf16[8,24,512]{2,1,0:T(8,128)(2,1)S(1)}, u32[]{:S(2)}, u32[]{:S(2)}) %all-to-all-start.1) | async-done | bytes 196640 | tf_op jit(solution)/shard_map/all_to_all | solution.py:456
  50.9 11.5 %all_to_all.21 = bf16[8,24,512]{2,1,0:T(8,128)(2,1)S(1)} all-to-all(bf16[8,24,512]{2,1,0:T(8,128)(2,1)S(1)} %depth_sum.1), channel_id=1, replica_groups={{224,192,160,128,96,64,32,0},{225,193,161,129,97,65,33,1},{226,194,162,..., dimensions={0} | all-to-all | bytes 393216 | tf_op jit(solution)/shard_map/all_to_all | solution.py:456
  62.4 1.1 spread.1
  63.4 6.3 %all-to-all-start.3 = ((bf16[8,128,512]{2,1,0:T(8,128)(2,1)}), bf16[8,128,512]{2,1,0:T(8,128)(2,1)S(1)}, u32[]{:S(2)}, u32[]{:S(2)}) async-start(bf16[8,128,512]{2,1,0:T(8,128)(2,1)} %get-tuple-element.26), calls=%async_computation.3 | async-start | bytes 2097152 | tf_op jit(solution)/shard_map/all_to_all | solution.py:456
  69.7 0.0 collective-permute-done.1.got_ref
  69.7 0.0 copy-start
  69.7 1.0 copy-done
  70.7 1.0 tail.1
  71.7 4.9 %collective-permute-start.2 = (bf16[2,128,512]{2,1,0:T(8,128)(2,1)S(1)}, bf16[2,128,512]{2,1,0:T(8,128)(2,1)S(1)}, u32[]{:S(2)}, u32[]{:S(2)}) collective-permute-start(bf16[2,128,512]{2,1,0:T(8,128)(2,1)S(1)} %tail.1), channel_id=1, source_target_pairs={{0,4},{4,8},{8,12},{12,16},{16,20},{20,24},{24,28},{28,32},{32,36}... | collective-permute-start | bytes 786440 | tf_op jit(solution)/shard_map/ppermute | solution.py:479
  76.6 0.6 collective-permute-start.9
  77.2 1.5 %collective-permute-start.8 = (bf16[64,512]{1,0:T(8,128)(2,1)S(1)}, bf16[64,512]{1,0:T(8,128)(2,1)S(1)}, u32[]{:S(2)}, u32[]{:S(2)}) collective-permute-start(bf16[64,512]{1,0:T(8,128)(2,1)S(1)} %get-tuple-element.28.rest_0_), channel_id=1, source_target_pairs={{0,8},{4,12},{8,16},{12,20},{16,24},{20,28},{24,0},{28,4},{1,9},{5... | collective-permute-start | bytes 196616 | tf_op jit(solution)/shard_map/ppermute | solution.py:485
  78.7 10.0 %collective-permute-done.2.halo_ref = bf16[2,128,512]{2,1,0:T(8,128)(2,1)S(1)} collective-permute-done((bf16[2,128,512]{2,1,0:T(8,128)(2,1)S(1)}, bf16[2,128,512]{2,1,0:T(8,128)(2,1)S(1)}, u32[]{:S(2)}, u32[]{:S(2)}) %collective-permute-start.2) | collective-permute-done | bytes 262176 | tf_op jit(solution)/shard_map/ppermute | solution.py:479
  88.7 4.3 %window_attention.1.att_ref = f32[512,512]{1,0:T(8,128)} custom-call(s32[1]{0:T(128)} %bitcast.place_ref, bf16[256,1024]{1,0:T(8,128)(2,1)} %own_q.1, bf16[256,1024]{1,0:T(8,128)(2,1)} %own_k.1, bf16[256,1024]{1,0:T(8,128)(2,1)} %own_v.1, bf16[4,256,512]{2,1,0:T(8,128)(2,1)} %copy-done, bf16[2,128,512]{2,1,0:T(8,128)(2,1)S(1)} %collective-permute-done.2.halo_ref), custom_call_target="tpu_custom_call" | custom-call | flops 268435456 | bytes 1572864 | tf_op jit(solution)/shard_map/window_attention/pallas_call | solution.py:299
  93.0 0.1 collective-permute-start.7
  93.1 4.4 %collective-permute-start.6 = (bf16[64,512]{1,0:T(8,128)(2,1)S(1)}, bf16[64,512]{1,0:T(8,128)(2,1)S(1)}, u32[]{:S(2)}, u32[]{:S(2)}) collective-permute-start(bf16[64,512]{1,0:T(8,128)(2,1)S(1)} %get-tuple-element.28.rest_0_), channel_id=1, source_target_pairs={{0,12},{4,8},{8,20},{12,16},{16,28},{20,24},{24,4},{28,0},{1,13},{... | collective-permute-start | bytes 196616 | tf_op jit(solution)/shard_map/ppermute | solution.py:485
  97.5 0.0 collective-permute-start.5
  97.5 0.0 collective-permute-done.9.rest_7_
  97.5 2.9 %collective-permute-start.4 = (bf16[64,512]{1,0:T(8,128)(2,1)S(1)}, bf16[64,512]{1,0:T(8,128)(2,1)S(1)}, u32[]{:S(2)}, u32[]{:S(2)}) collective-permute-start(bf16[64,512]{1,0:T(8,128)(2,1)S(1)} %get-tuple-element.28.rest_0_), channel_id=1, source_target_pairs={{0,20},{4,16},{8,28},{12,24},{16,4},{20,0},{24,12},{28,8},{1,21},{... | collective-permute-start | bytes 196616 | tf_op jit(solution)/shard_map/ppermute | solution.py:485
  100.4 0.0 collective-permute-done.8.rest_6_
  100.4 3.6 %collective-permute-start.3 = (bf16[64,512]{1,0:T(8,128)(2,1)S(1)}, bf16[64,512]{1,0:T(8,128)(2,1)S(1)}, u32[]{:S(2)}, u32[]{:S(2)}) collective-permute-start(bf16[64,512]{1,0:T(8,128)(2,1)S(1)} %get-tuple-element.28.rest_0_), channel_id=1, source_target_pairs={{0,4},{4,0},{8,12},{12,8},{16,20},{20,16},{24,28},{28,24},{1,5},{5... | collective-permute-start | bytes 196616 | tf_op jit(solution)/shard_map/ppermute | solution.py:485
  104.0 0.0 all-to-all-done.3
  104.0 5.1 %open_answer.1.hidden_ref = bf16[512,512]{1,0:T(8,128)(2,1)S(1)} custom-call(s32[1]{0:T(128)} %bitcast.place_ref, bf16[8,2,64,512]{3,2,1,0:T(8,128)(2,1)S(1)} %bitcast.7, bf16[2,512,512]{2,1,0:T(8,128)(2,1)} %gate_ref.1, bf16[2,512,512]{2,1,0:T(8,128)(2,1)} %up_ref.1, bf16[256,1024]{1,0:T(8,128)(2,1)} %own_ref.1, bf16[4,256,512]{2,1,0:T(8,128)(2,1)} %copy-done), custom_call_target="tpu_custom_call" | custom-call | flops 3758096384 | bytes 3145728 | tf_op jit(solution)/shard_map/open_answer/pallas_call | solution.py:373
  109.1 0.0 collective-permute-done.7.rest_5_
  109.1 0.0 collective-permute-done.6.rest_4_
  109.1 0.0 collective-permute-done.5.rest_3_
  109.1 0.0 collective-permute-done.4.rest_2_
  109.1 0.0 collective-permute-done.3.rest_1_
  109.1 3.3 %close_answer.1 = (bf16[128,512]{1,0:T(8,128)(2,1)S(1)}, bf16[128,512]{1,0:T(8,128)(2,1)S(1)}, bf16[128,512]{1,0:T(8,128)(2,1)S(1)}, bf16[128,512]{1,0:T(8,128)(2,1)S(1)}) custom-call(s32[1]{0:T(128)} %bitcast.place_ref, bf16[2,512,512]{2,1,0:T(8,128)(2,1)} %down_ref.1, bf16[512,512]{1,0:T(8,128)(2,1)S(1)} %open_answer.1.hidden_ref, ...), custom_call_target="tpu_custom_call" | custom-call | flops 1879048192 | bytes 2097152 | tf_op jit(solution)/shard_map/close_answer/pallas_call | solution.py:412
  112.5 0.1 collective-permute-start.10
  112.6 0.8 collective-permute-start.11
  113.3 1.1 collective-permute-start.12
  114.4 0.0 collective-permute-done.10.refs_1_
  114.4 4.6 %collective-permute-done.11.refs_2_ = bf16[128,512]{1,0:T(8,128)(2,1)S(1)} collective-permute-done((bf16[128,512]{1,0:T(8,128)(2,1)S(1)}, bf16[128,512]{1,0:T(8,128)(2,1)S(1)}, u32[]{:S(2)}, u32[]{:S(2)}) %collective-permute-start.11) | collective-permute-done | bytes 131104 | tf_op jit(solution)/shard_map/ppermute | solution.py:490
  119.0 1.7 %collective-permute-done.12.refs_3_ = bf16[128,512]{1,0:T(8,128)(2,1)S(1)} collective-permute-done((bf16[128,512]{1,0:T(8,128)(2,1)S(1)}, bf16[128,512]{1,0:T(8,128)(2,1)S(1)}, u32[]{:S(2)}, u32[]{:S(2)}) %collective-permute-start.12) | collective-permute-done | bytes 131104 | tf_op jit(solution)/shard_map/ppermute | solution.py:491
  120.7 0.9 unpack.1
  (1 shorter events, 0.0 us)
Async XLA Ops:
  1.3 2.0 %collective-permute-start = (bf16[2,256,512]{2,1,0:T(8,128)(2,1)S(1)}, bf16[2,256,512]{2,1,0:T(8,128)(2,1)S(1)}, u32[]{:S(2)}, u32[]{:S(2)}) collective-permute-start(bf16[2,256,512]{2,1,0:T(8,128)(2,1)S(1)} %get-tuple-element.21), channel_id=1, source_target_pairs={{0,2},{2,0},{1,3},{3,1},{4,6},{6,4},{5,7},{7,5},{8,10},{10,8},{9,1... | collective-permute-start | bytes 1572872 | tf_op jit(solution)/shard_map/ppermute | solution.py:468
  34.6 16.3 %all-to-all-start.1 = ((bf16[8,24,512]{2,1,0:T(8,128)(2,1)}), bf16[8,24,512]{2,1,0:T(8,128)(2,1)S(1)}, u32[]{:S(2)}, u32[]{:S(2)}) async-start(bf16[8,24,512]{2,1,0:T(8,128)(2,1)} %bitcast.3), calls=%async_computation.1 | async-start | bytes 393216 | tf_op jit(solution)/shard_map/all_to_all | solution.py:456
  43.8 26.0 %collective-permute-start.1 = (bf16[4,256,512]{2,1,0:T(8,128)(2,1)S(1)}, bf16[4,256,512]{2,1,0:T(8,128)(2,1)S(1)}, u32[]{:S(2)}, u32[]{:S(2)}) collective-permute-start(bf16[4,256,512]{2,1,0:T(8,128)(2,1)S(1)} %get-tuple-element.27), channel_id=1, source_target_pairs={{0,2},{2,0},{1,3},{3,1},{4,6},{6,4},{5,7},{7,5},{8,10},{10,8},{9,1... | collective-permute-start | bytes 3145736 | tf_op jit(solution)/shard_map/ppermute | solution.py:470
  63.4 40.6 %all-to-all-start.3 = ((bf16[8,128,512]{2,1,0:T(8,128)(2,1)}), bf16[8,128,512]{2,1,0:T(8,128)(2,1)S(1)}, u32[]{:S(2)}, u32[]{:S(2)}) async-start(bf16[8,128,512]{2,1,0:T(8,128)(2,1)} %get-tuple-element.26), calls=%async_computation.3 | async-start | bytes 2097152 | tf_op jit(solution)/shard_map/all_to_all | solution.py:456
  69.7 1.0 copy-start
  71.7 17.0 %collective-permute-start.2 = (bf16[2,128,512]{2,1,0:T(8,128)(2,1)S(1)}, bf16[2,128,512]{2,1,0:T(8,128)(2,1)S(1)}, u32[]{:S(2)}, u32[]{:S(2)}) collective-permute-start(bf16[2,128,512]{2,1,0:T(8,128)(2,1)S(1)} %tail.1), channel_id=1, source_target_pairs={{0,4},{4,8},{8,12},{12,16},{16,20},{20,24},{24,28},{28,32},{32,36}... | collective-permute-start | bytes 786440 | tf_op jit(solution)/shard_map/ppermute | solution.py:479
  76.6 20.9 %collective-permute-start.9 = (bf16[64,512]{1,0:T(8,128)(2,1)S(1)}, bf16[64,512]{1,0:T(8,128)(2,1)S(1)}, u32[]{:S(2)}, u32[]{:S(2)}) collective-permute-start(bf16[64,512]{1,0:T(8,128)(2,1)S(1)} %get-tuple-element.28.rest_0_), channel_id=1, source_target_pairs={{0,24},{4,28},{8,0},{12,4},{16,8},{20,12},{24,16},{28,20},{1,25},{... | collective-permute-start | bytes 196616 | tf_op jit(solution)/shard_map/ppermute | solution.py:485
  77.2 23.1 %collective-permute-start.8 = (bf16[64,512]{1,0:T(8,128)(2,1)S(1)}, bf16[64,512]{1,0:T(8,128)(2,1)S(1)}, u32[]{:S(2)}, u32[]{:S(2)}) collective-permute-start(bf16[64,512]{1,0:T(8,128)(2,1)S(1)} %get-tuple-element.28.rest_0_), channel_id=1, source_target_pairs={{0,8},{4,12},{8,16},{12,20},{16,24},{20,28},{24,0},{28,4},{1,9},{5... | collective-permute-start | bytes 196616 | tf_op jit(solution)/shard_map/ppermute | solution.py:485
  93.0 16.1 %collective-permute-start.7 = (bf16[64,512]{1,0:T(8,128)(2,1)S(1)}, bf16[64,512]{1,0:T(8,128)(2,1)S(1)}, u32[]{:S(2)}, u32[]{:S(2)}) collective-permute-start(bf16[64,512]{1,0:T(8,128)(2,1)S(1)} %get-tuple-element.28.rest_0_), channel_id=1, source_target_pairs={{0,28},{4,24},{8,4},{12,0},{16,12},{20,8},{24,20},{28,16},{1,29},{... | collective-permute-start | bytes 196616 | tf_op jit(solution)/shard_map/ppermute | solution.py:485
  93.1 16.0 %collective-permute-start.6 = (bf16[64,512]{1,0:T(8,128)(2,1)S(1)}, bf16[64,512]{1,0:T(8,128)(2,1)S(1)}, u32[]{:S(2)}, u32[]{:S(2)}) collective-permute-start(bf16[64,512]{1,0:T(8,128)(2,1)S(1)} %get-tuple-element.28.rest_0_), channel_id=1, source_target_pairs={{0,12},{4,8},{8,20},{12,16},{16,28},{20,24},{24,4},{28,0},{1,13},{... | collective-permute-start | bytes 196616 | tf_op jit(solution)/shard_map/ppermute | solution.py:485
  97.5 11.6 %collective-permute-start.5 = (bf16[64,512]{1,0:T(8,128)(2,1)S(1)}, bf16[64,512]{1,0:T(8,128)(2,1)S(1)}, u32[]{:S(2)}, u32[]{:S(2)}) collective-permute-start(bf16[64,512]{1,0:T(8,128)(2,1)S(1)} %get-tuple-element.28.rest_0_), channel_id=1, source_target_pairs={{0,16},{4,20},{8,24},{12,28},{16,0},{20,4},{24,8},{28,12},{1,17},{... | collective-permute-start | bytes 196616 | tf_op jit(solution)/shard_map/ppermute | solution.py:485
  97.5 11.6 %collective-permute-start.4 = (bf16[64,512]{1,0:T(8,128)(2,1)S(1)}, bf16[64,512]{1,0:T(8,128)(2,1)S(1)}, u32[]{:S(2)}, u32[]{:S(2)}) collective-permute-start(bf16[64,512]{1,0:T(8,128)(2,1)S(1)} %get-tuple-element.28.rest_0_), channel_id=1, source_target_pairs={{0,20},{4,16},{8,28},{12,24},{16,4},{20,0},{24,12},{28,8},{1,21},{... | collective-permute-start | bytes 196616 | tf_op jit(solution)/shard_map/ppermute | solution.py:485
  100.4 8.8 %collective-permute-start.3 = (bf16[64,512]{1,0:T(8,128)(2,1)S(1)}, bf16[64,512]{1,0:T(8,128)(2,1)S(1)}, u32[]{:S(2)}, u32[]{:S(2)}) collective-permute-start(bf16[64,512]{1,0:T(8,128)(2,1)S(1)} %get-tuple-element.28.rest_0_), channel_id=1, source_target_pairs={{0,4},{4,0},{8,12},{12,8},{16,20},{20,16},{24,28},{28,24},{1,5},{5... | collective-permute-start | bytes 196616 | tf_op jit(solution)/shard_map/ppermute | solution.py:485
  112.5 2.0 %collective-permute-start.10 = (bf16[128,512]{1,0:T(8,128)(2,1)S(1)}, bf16[128,512]{1,0:T(8,128)(2,1)S(1)}, u32[]{:S(2)}, u32[]{:S(2)}) collective-permute-start(bf16[128,512]{1,0:T(8,128)(2,1)S(1)} %get-tuple-element.30), channel_id=1, source_target_pairs={{0,2},{2,0},{1,3},{3,1},{4,6},{6,4},{5,7},{7,5},{8,10},{10,8},{9,1... | collective-permute-start | bytes 393224 | tf_op jit(solution)/shard_map/ppermute | solution.py:492
  112.6 6.5 %collective-permute-start.11 = (bf16[128,512]{1,0:T(8,128)(2,1)S(1)}, bf16[128,512]{1,0:T(8,128)(2,1)S(1)}, u32[]{:S(2)}, u32[]{:S(2)}) collective-permute-start(bf16[128,512]{1,0:T(8,128)(2,1)S(1)} %get-tuple-element.31), channel_id=1, source_target_pairs={{0,1},{1,0},{2,3},{3,2},{4,5},{5,4},{6,7},{7,6},{8,9},{9,8},{10,11... | collective-permute-start | bytes 393224 | tf_op jit(solution)/shard_map/ppermute | solution.py:490
  113.3 7.4 %collective-permute-start.12 = (bf16[128,512]{1,0:T(8,128)(2,1)S(1)}, bf16[128,512]{1,0:T(8,128)(2,1)S(1)}, u32[]{:S(2)}, u32[]{:S(2)}) collective-permute-start(bf16[128,512]{1,0:T(8,128)(2,1)S(1)} %get-tuple-element.32), channel_id=1, source_target_pairs={{0,3},{1,2},{2,1},{3,0},{4,7},{5,6},{6,5},{7,4},{8,11},{9,10},{10,... | collective-permute-start | bytes 393224 | tf_op jit(solution)/shard_map/ppermute | solution.py:491
